TPU v7x, 256 devices: a whole 4x4x8 slice. The times are simulated.
256 devices in a mesh: emit: 8 (over y, z_hi), client: 32 (over x, z_lo, core).
Axes of the slice: x: 4, y: 4, z: 8 (z_hi: 2, z_lo: 4; z = z_hi * 4 + z_lo), core: 2. Of those that a mesh axis runs over, the one named last changes fastest.
Arguments:
- features: bfloat16 [131072, 768], P('client'), may hold values from -28 to 28
- labels: int32 [131072], P('client'), may hold values from 0 to 999
- client_ids: int32 [256], replicated, may hold values from 0 to 255, each once
- trunk_in: bfloat16 [256, 2048], replicated, may hold values from -6 to 6
- trunk_weight: bfloat16 [2048, 2048], P(None, 'client'), may hold values from -0.125 to 0.125
- class_table: bfloat16 [1000, 2048], P('emit'), may hold values from -6 to 6
- emit_weight: bfloat16 [2048, 768], P('emit'), may hold values from -0.125 to 0.125
Outputs:
- loss: float32 [131072], P('client')
- emit_grad: float32 [2048, 768], P(('emit', 'client'))
- trunk_grad: float32 [2048, 2048], P(None, ('emit', 'client'))
Inputs may be any that keep to these rules, and one draw needn't show every extreme that they name: Each client number appears once; slot s holds the features of client client_ids[s].
All inputs are finite; a program needn't handle non-finite values.
Results may differ from a plain program's by a relative error of at most 0.022.
Values may be sent and summed in bfloat16 or wider, within the bound.
A program may use at most 128 MiB of HBM per device.

v0:
```python
import jax
import jax.numpy as jnp
from jax import lax
from jax.sharding import PartitionSpec as P

CL_DEV = 8


def sent_to_all(x, axis):
    count = lax.axis_size(axis)
    return lax.all_to_all(jnp.broadcast_to(x[None], (count, *x.shape)), axis, 0, 0, tiled=True)


def laid_out(parts, dim):
    parts = jnp.moveaxis(parts, 0, dim)
    lengths = parts.shape
    return parts.reshape(*lengths[:dim], lengths[dim] * lengths[dim + 1], *lengths[dim + 2 :])


def gather_directly(x, axis, dim):
    parts = sent_to_all(x, axis)
    return laid_out(parts, dim)


def taken_together(x, axis):
    everything = sent_to_all(x, axis)
    return jnp.max(everything, axis=0)


def of_everyone(x, axis):
    return sent_to_all(x, axis).astype(jnp.float32).sum(axis=0)


def in_blocks(x, dim, count):
    lengths = x.shape
    parts = x.reshape(*lengths[:dim], count, lengths[dim] // count, *lengths[dim + 1 :])
    return jnp.moveaxis(parts, dim, 0)


def sum_at_owner(x, axis, dim):
    parts = in_blocks(x, dim, lax.axis_size(axis))
    arrived = lax.all_to_all(parts, axis, split_axis=0, concat_axis=0, tiled=True)
    return arrived.astype(jnp.float32).sum(axis=0)


def silu_grad(value):
    sig = jax.nn.sigmoid(value)
    return sig * (1.0 + value * (1.0 - sig))


def per_device(features, labels, client_ids, trunk_in, trunk_weight, class_table, emit_weight):
    slots = CL_DEV
    clients = trunk_in.shape[0]
    hidden_dim = trunk_in.shape[1]
    classes = class_table.shape[0]
    feat_dim = features.shape[1]
    samples = features.shape[0] // slots
    client_index = lax.axis_index("client")
    emit_index = lax.axis_index("emit")
    pre_cols = jnp.dot(trunk_in, trunk_weight, preferred_element_type=jnp.float32).astype(
        jnp.bfloat16
    )
    pre_all = gather_directly(pre_cols, "client", 1)
    own_ids = lax.dynamic_slice_in_dim(client_ids, client_index * slots, slots)
    numbers = lax.iota(jnp.int32, clients)
    picker = (own_ids[:, None] == numbers[None, :]).astype(jnp.bfloat16)
    pre_own = jnp.dot(picker, pre_all, preferred_element_type=jnp.float32)
    code_in = jax.nn.silu(pre_own)[:, None, :] + class_table.astype(jnp.float32)[None, :, :]
    code = jax.nn.silu(code_in).astype(jnp.bfloat16).reshape(slots * classes, hidden_dim)
    emit_full = lax.all_gather(emit_weight, "emit", axis=0, tiled=True)
    heads = jnp.dot(code, emit_full, preferred_element_type=jnp.float32).astype(jnp.bfloat16)
    heads = heads.reshape(slots, classes, feat_dim)
    feats = features.reshape(slots, samples, feat_dim)
    logits = jnp.einsum("snd,skd->snk", feats, heads, preferred_element_type=jnp.float32)
    class_ids = emit_index * classes + lax.iota(jnp.int32, classes)
    onehot = (labels.reshape(slots, samples)[:, :, None] == class_ids[None, None, :]).astype(
        jnp.float32
    )
    target = jnp.sum(logits * onehot, axis=2)
    local_top = jnp.max(logits, axis=2)
    top = taken_together(local_top, "emit")
    expd = jnp.exp(logits - top[:, :, None])
    total, target_all = (
        of_everyone(jnp.sum(expd, axis=2).astype(jnp.bfloat16), "emit").astype(jnp.float32),
        of_everyone(target.astype(jnp.bfloat16), "emit").astype(jnp.float32),
    )
    loss = (top + jnp.log(total) - target_all).reshape(slots * samples)
    grad_logits = ((expd / total[:, :, None] - onehot) / clients).astype(jnp.bfloat16)
    grad_heads = jnp.einsum("snk,snd->skd", grad_logits, feats, preferred_element_type=jnp.float32)
    grad_heads = grad_heads.astype(jnp.bfloat16).reshape(slots * classes, feat_dim)
    partial_rows = lax.psum_scatter(
        jnp.einsum("rh,rd->hd", code, grad_heads, preferred_element_type=jnp.float32).astype(
            jnp.bfloat16
        ),
        "emit",
        scatter_dimension=0,
        tiled=True,
    )
    emit_grad = sum_at_owner(partial_rows, "client", 0)
    grad_code = jnp.dot(grad_heads, emit_full.T, preferred_element_type=jnp.float32)
    grad_code = grad_code.reshape(slots, classes, hidden_dim)
    grad_sum = jnp.sum(grad_code * silu_grad(code_in), axis=1)
    block = hidden_dim // lax.axis_size("emit")
    grad_block = sum_at_owner(grad_sum.astype(jnp.bfloat16), "emit", 1)
    pre_block = lax.dynamic_slice_in_dim(pre_own, emit_index * block, block, 1)
    grad_pre = (grad_block * silu_grad(pre_block)).astype(jnp.bfloat16)
    grad_all = gather_directly(grad_pre, "client", 0)
    width = block // lax.axis_size("client")
    grad_mine = lax.dynamic_slice_in_dim(grad_all, client_index * width, width, 1)
    picker_all = (client_ids[:, None] == numbers[None, :]).astype(jnp.bfloat16)
    grad_client = jnp.einsum(
        "sc,sw->cw", picker_all, grad_mine, preferred_element_type=jnp.float32
    ).astype(jnp.bfloat16)
    trunk_grad = jnp.einsum("ch,cw->hw", trunk_in, grad_client, preferred_element_type=jnp.float32)
    return (loss, emit_grad, trunk_grad)


def solution(mesh):
    return jax.shard_map(
        per_device,
        mesh=mesh,
        in_specs=(
            P("client", None),
            P("client"),
            P(),
            P(),
            P(None, "client"),
            P("emit", None),
            P("emit", None),
        ),
        out_specs=(P("client"), P(("emit", "client"), None), P(None, ("emit", "client"))),
        check_vma=False,
    )
```

profile of v0, /device:TPU:1, one launch (start us, length us, event | category | flops | bytes accessed | tf_op | source)
XLA Modules:
  0.0 302.1 jit_solution(12591394443601378770)
XLA Ops:
  7.2 0.7 all-gather.2.cloned.1.call-update
  8.4 1.4 convolution_convert_fusion.1
  9.8 1.1 broadcast_in_dim.10
  10.9 10.0 %all-to-all-start = ((bf16[32,256,64]{1,2,0:T(8,128)(2,1)}), bf16[32,256,64]{1,2,0:T(8,128)(2,1)S(1)}, u32[]{:S(2)}, u32[]{:S(2)}) async-start(bf16[32,256,64]{1,2,0:T(8,128)(2,1)} %broadcast_in_dim.10), calls=%async_computation | async-start | bytes 2097152 | tf_op jit(solution)/shard_map/all_to_all | solution.py:11
  20.9 1.1 convert_element_type.69
  22.2 35.0 %all-to-all-done = bf16[32,256,64]{1,2,0:T(8,128)(2,1)S(1)} async-done(((bf16[32,256,64]{1,2,0:T(8,128)(2,1)}), bf16[32,256,64]{1,2,0:T(8,128)(2,1)S(1)}, u32[]{:S(2)}, u32[]{:S(2)}) %all-to-all-start) | async-done | bytes 1048608 | tf_op jit(solution)/shard_map/all_to_all | solution.py:11
  57.6 4.3 %broadcast_add_fusion = f32[8,125,2048]{2,1,0:T(8,128)} fusion(f32[125,2048]{1,0:T(8,128)S(1)} %convert_element_type.69, f32[8,2048]{1,0:T(8,128)S(1)} %get-tuple-element.5), kind=kLoop, calls=%fused_computation.16 | loop fusion | flops 2048000 | bytes 9281536 | tf_op jit(solution)/shard_map/add | solution.py:68
  61.9 7.9 %add.67 = f32[1000,2048]{1,0:T(8,128)} reshape(f32[8,125,2048]{2,1,0:T(8,128)} %broadcast_add_fusion) | data formatting | bytes 16384000 | tf_op jit(solution)/shard_map/add | solution.py:68
  69.8 41.8 %all-gather.2.cloned.1.call-done = bf16[2048,768]{1,0:T(8,128)(2,1)} async-done(((bf16[256,768]{1,0:T(8,128)(2,1)}), bf16[2048,768]{1,0:T(8,128)(2,1)}) %all-gather.2.cloned.1.call-update) | async-done | bytes 3145744 | tf_op jit(solution)/shard_map/all_gather | solution.py:70
  111.6 8.6 %fusion.23 = bf16[1000,768]{1,0:T(8,128)(2,1)S(1)} fusion(bf16[2048,768]{1,0:T(8,128)(2,1)} %all-gather.2.cloned.1.call-done, f32[1000,2048]{1,0:T(8,128)} %add.67), kind=kOutput, calls=%fused_computation.32 | convolution fusion | flops 3156736000 | bytes 12873728 | tf_op jit(solution)/shard_map/dot_general | solution.py:71
  120.2 1.6 reshape.60
  121.8 5.4 %bitcast_reduce_fusion = (f32[8,512]{1,0:T(8,128)S(1)}, f32[8,125,512]{2,1,0:T(8,128)S(1)}) fusion(bf16[8,125,768]{2,1,0:T(8,128)(2,1)} %reshape.60, bf16[8,512,768]{2,1,0:T(8,128)(2,1)} %bitcast.40), kind=kOutput, calls=%fused_computation.28 | convolution fusion | flops 786939904 | bytes 9891840 | tf_op jit(solution)/shard_map/snd,skd->snk/dot_general | solution.py:74
  127.3 0.6 broadcast_in_dim.11
  127.9 3.4 %all-to-all-start.1 = ((f32[8,8,512]{2,1,0:T(8,128)}), f32[8,8,512]{2,1,0:T(8,128)S(1)}, u32[]{:S(2)}, u32[]{:S(2)}) async-start(f32[8,8,512]{2,1,0:T(8,128)} %broadcast_in_dim.11), calls=%async_computation.1 | async-start | bytes 262144 | tf_op jit(solution)/shard_map/all_to_all | solution.py:11
  131.4 9.3 %all-to-all-done.1 = f32[8,8,512]{2,1,0:T(8,128)S(1)} async-done(((f32[8,8,512]{2,1,0:T(8,128)}), f32[8,8,512]{2,1,0:T(8,128)S(1)}, u32[]{:S(2)}, u32[]{:S(2)}) %all-to-all-start.1) | async-done | bytes 131104 | tf_op jit(solution)/shard_map/all_to_all | solution.py:11
  141.3 11.5 %all_to_all.35 = bf16[8,8,512]{2,1,0:T(8,128)(2,1)S(1)} all-to-all(bf16[8,8,512]{2,1,0:T(8,128)(2,1)S(1)} %broadcast_in_dim.12), channel_id=1, replica_groups=mesh['emit'=8,'client'=32] {'emit'}, dimensions={0} | all-to-all | bytes 131072 | tf_op jit(solution)/shard_map/all_to_all | solution.py:11
  152.8 4.1 %convolution_convert_fusion = bf16[8,125,768]{2,1,0:T(8,128)(2,1)S(1)} fusion(bf16[8,512,768]{2,1,0:T(8,128)(2,1)} %bitcast.41, f32[8,125,512]{2,1,0:T(8,128)S(1)} %get-tuple-element.8, f32[8,512]{1,0:T(8,128)S(1)} %convert_reduce_fusion.2, s32[8,512]{1,0:T(8,128)S(1)} %eq.44, f32[8,512]{1,0:T(8,128)S(1)} %reduce_max.19, s32[125]{0:T(128)S(1)} %iota_add_fusion), kind=kOutput, calls=%fused_computation.31 | convolution fusion | flops 790784000 | bytes 9925108 | tf_op jit(solution)/shard_map/snk,snd->skd/dot_general | solution.py:89
  156.9 1.1 copy-done.6
  158.1 5.7 %bitcast_convert_fusion = bf16[2048,768]{1,0:T(8,128)(2,1)} fusion(bf16[8,125,768]{2,1,0:T(8,128)(2,1)S(1)} %convolution_convert_fusion, f32[125,2048]{1,0:T(8,128)S(1)} %copy-done.2, f32[8,2048]{1,0:T(8,128)S(1)} %get-tuple-element.5), kind=kOutput, calls=%fused_computation.12 | convolution fusion | flops 3159588864 | bytes 5771264 | tf_op jit(solution)/shard_map/rh,rd->hd/dot_general | solution.py:92
  163.8 8.1 %fusion.7 = bf16[8,2048]{1,0:T(8,128)(2,1)} fusion(bf16[8,125,768]{2,1,0:T(8,128)(2,1)} %copy-done.6, f32[125,2048]{1,0:T(8,128)S(1)} %copy-done.3, f32[8,2048]{1,0:T(8,128)S(1)} %get-tuple-element.5, bf16[2048,768]{1,0:T(8,128)(2,1)} %all-gather.2.cloned.1.call-done), kind=kOutput, calls=%fused_computation.10 | convolution fusion | flops 3166191616 | bytes 5804032 | tf_op jit(solution)/shard_map/dot_general | solution.py:100
  172.0 3.3 %all-to-all-start.5 = ((bf16[8,8,256]{2,1,0:T(8,128)(2,1)}), bf16[8,8,256]{2,1,0:T(8,128)(2,1)S(1)}, u32[]{:S(2)}, u32[]{:S(2)}) async-start(bf16[8,8,256]{2,1,0:T(8,128)(2,1)} %bitcast.8), calls=%async_computation.6 | async-start | bytes 65536 | tf_op jit(solution)/shard_map/all_to_all | solution.py:42
  175.3 9.0 %all-to-all-done.5 = bf16[8,8,256]{2,1,0:T(8,128)(2,1)S(1)} async-done(((bf16[8,8,256]{2,1,0:T(8,128)(2,1)}), bf16[8,8,256]{2,1,0:T(8,128)(2,1)S(1)}, u32[]{:S(2)}, u32[]{:S(2)}) %all-to-all-start.5) | async-done | bytes 32800 | tf_op jit(solution)/shard_map/all_to_all | solution.py:42
  184.4 0.6 broadcast_in_dim.13
  185.0 3.4 %all-to-all-start.3 = ((bf16[8,8,512]{2,1,0:T(8,128)(2,1)}), bf16[8,8,512]{2,1,0:T(8,128)(2,1)S(1)}, u32[]{:S(2)}, u32[]{:S(2)}) async-start(bf16[8,8,512]{2,1,0:T(8,128)(2,1)} %broadcast_in_dim.13), calls=%async_computation.3 | async-start | bytes 131072 | tf_op jit(solution)/shard_map/all_to_all | solution.py:11
  188.4 9.4 %all-to-all-done.3 = bf16[8,8,512]{2,1,0:T(8,128)(2,1)S(1)} async-done(((bf16[8,8,512]{2,1,0:T(8,128)(2,1)}), bf16[8,8,512]{2,1,0:T(8,128)(2,1)S(1)}, u32[]{:S(2)}, u32[]{:S(2)}) %all-to-all-start.3) | async-done | bytes 65568 | tf_op jit(solution)/shard_map/all_to_all | solution.py:11
  197.8 25.7 %all_to_all.36 = bf16[32,8,256]{2,1,0:T(8,128)(2,1)S(1)} all-to-all(bf16[32,8,256]{2,1,0:T(8,128)(2,1)S(1)} %broadcast_in_dim.14), channel_id=1, replica_groups=mesh['emit'=8,'client'=32] {'client'}, dimensions={0} | all-to-all | bytes 262144 | tf_op jit(solution)/shard_map/all_to_all | solution.py:11
  223.5 50.2 %reduce-scatter.2.cloned.1.call-done = bf16[256,768]{1,0:T(8,128)(2,1)} async-done(((bf16[2048,768]{1,0:T(8,128)(2,1)}), bf16[256,768]{1,0:T(8,128)(2,1)}) %reduce-scatter.2.cloned.1.call-update) | async-done | bytes 393232 | tf_op jit(solution)/shard_map/reduce_scatter | solution.py:91
  273.7 6.8 %all-to-all-start.4 = ((bf16[32,8,768]{2,1,0:T(8,128)(2,1)}), bf16[32,8,768]{2,1,0:T(8,128)(2,1)S(1)}, u32[]{:S(2)}, u32[]{:S(2)}) async-start(bf16[32,8,768]{2,1,0:T(8,128)(2,1)} %bitcast.43), calls=%async_computation.5 | async-start | bytes 786432 | tf_op jit(solution)/shard_map/all_to_all | solution.py:42
  280.6 0.6 copy.15
  281.2 1.1 convolution_bitcast_fusion
  282.3 12.3 %all-to-all-done.4 = bf16[32,8,768]{2,1,0:T(8,128)(2,1)S(1)} async-done(((bf16[32,8,768]{2,1,0:T(8,128)(2,1)}), bf16[32,8,768]{2,1,0:T(8,128)(2,1)S(1)}, u32[]{:S(2)}, u32[]{:S(2)}) %all-to-all-start.4) | async-done | bytes 393248 | tf_op jit(solution)/shard_map/all_to_all | solution.py:42
  294.6 0.7 convert_reduce_fusion
  (29 shorter events, 1.7 us)
Async XLA Ops:
  7.2 1.2 copy-start
  7.2 14.9 %copy-start.5 = (s32[256]{0:T(256)S(1)}, s32[256]{0:T(256)}, u32[]{:S(2)}) copy-start(s32[256]{0:T(256)} %param.9) | copy-start | bytes 3076
  7.2 104.4 %all-gather.2.cloned.1.call-start = ((), (), s32[]{:S(2)}) async-start(), calls=%async_computation.8 | async-start | bytes 3538944 | tf_op jit(solution)/shard_map/all_gather | solution.py:70
  10.9 46.3 %all-to-all-start = ((bf16[32,256,64]{1,2,0:T(8,128)(2,1)}), bf16[32,256,64]{1,2,0:T(8,128)(2,1)S(1)}, u32[]{:S(2)}, u32[]{:S(2)}) async-start(bf16[32,256,64]{1,2,0:T(8,128)(2,1)} %broadcast_in_dim.10), calls=%async_computation | async-start | bytes 2097152 | tf_op jit(solution)/shard_map/all_to_all | solution.py:11
  22.1 39.8 %copy-start.1 = (f32[125,2048]{1,0:T(8,128)}, f32[125,2048]{1,0:T(8,128)S(1)}, u32[]{:S(2)}) copy-start(f32[125,2048]{1,0:T(8,128)S(1)} %convert_element_type.69) | copy-start | bytes 3072004
  121.8 9.5 %copy-start.4 = (s32[4096]{0:T(1024)S(1)}, s32[4096]{0:T(1024)}, u32[]{:S(2)}) copy-start(s32[4096]{0:T(1024)} %param.8) | copy-start | bytes 49156
  127.9 12.8 %all-to-all-start.1 = ((f32[8,8,512]{2,1,0:T(8,128)}), f32[8,8,512]{2,1,0:T(8,128)S(1)}, u32[]{:S(2)}, u32[]{:S(2)}) async-start(f32[8,8,512]{2,1,0:T(8,128)} %broadcast_in_dim.11), calls=%async_computation.1 | async-start | bytes 262144 | tf_op jit(solution)/shard_map/all_to_all | solution.py:11
  131.3 142.4 %reduce-scatter.2.cloned.1.call-start = ((), (), s32[]{:S(2)}) async-start(), calls=%async_computation.9 | async-start | bytes 3538944 | tf_op jit(solution)/shard_map/reduce_scatter | solution.py:91
  152.8 5.3 %copy-start.2 = (f32[125,2048]{1,0:T(8,128)S(1)}, f32[125,2048]{1,0:T(8,128)}, u32[]{:S(2)}) copy-start(f32[125,2048]{1,0:T(8,128)} %copy-done.1) | copy-start | bytes 3072004
  156.9 1.1 copy-start.6
  158.1 5.8 %copy-start.3 = (f32[125,2048]{1,0:T(8,128)S(1)}, f32[125,2048]{1,0:T(8,128)}, u32[]{:S(2)}) copy-start(f32[125,2048]{1,0:T(8,128)} %copy-done.1) | copy-start | bytes 3072004
  172.0 12.4 %all-to-all-start.5 = ((bf16[8,8,256]{2,1,0:T(8,128)(2,1)}), bf16[8,8,256]{2,1,0:T(8,128)(2,1)S(1)}, u32[]{:S(2)}, u32[]{:S(2)}) async-start(bf16[8,8,256]{2,1,0:T(8,128)(2,1)} %bitcast.8), calls=%async_computation.6 | async-start | bytes 65536 | tf_op jit(solution)/shard_map/all_to_all | solution.py:42
  185.0 12.8 %all-to-all-start.3 = ((bf16[8,8,512]{2,1,0:T(8,128)(2,1)}), bf16[8,8,512]{2,1,0:T(8,128)(2,1)S(1)}, u32[]{:S(2)}, u32[]{:S(2)}) async-start(bf16[8,8,512]{2,1,0:T(8,128)(2,1)} %broadcast_in_dim.13), calls=%async_computation.3 | async-start | bytes 131072 | tf_op jit(solution)/shard_map/all_to_all | solution.py:11
  273.7 20.9 %all-to-all-start.4 = ((bf16[32,8,768]{2,1,0:T(8,128)(2,1)}), bf16[32,8,768]{2,1,0:T(8,128)(2,1)S(1)}, u32[]{:S(2)}, u32[]{:S(2)}) async-start(bf16[32,8,768]{2,1,0:T(8,128)(2,1)} %bitcast.43), calls=%async_computation.5 | async-start | bytes 786432 | tf_op jit(solution)/shard_map/all_to_all | solution.py:42
Sparse Core Ops, SparseCore 0:
  10.6 100.9 all-gather.1
  164.0 109.7 reduce-scatter.1
where the time goes:
time: 303 us; the launch traced here: 302 us
  waiting for transfers between devices  168 us (55%)
  blocking collectives  37.2 us (12%)
  matrix products  34.9 us (12%)
  starting transfers between devices  27 us (9%)
  local copies, waits for them, and re-layouts  14.3 us (5%)
  between operations  14.3 us (5%)
  other arithmetic  6.74 us (2%)
    all_to_all x3, waiting for transfers between devices, sent_to_all(): lax.all_to_all(jnp.broadcast_to(x[None], (count, *x.shape)), axis, 0, 0,...  53.7 us
    reduce_scatter x1, waiting for transfers between devices, per_device(): lax.psum_scatter(jnp.einsum('rh,rd->hd', code, grad_heads, preferred_elem...  50.2 us
    all_gather x1, waiting for transfers between devices, per_device(): emit_full = lax.all_gather(emit_weight, 'emit', axis=0, tiled=True)  41.8 us
    all_to_all x2, blocking collectives, sent_to_all(): lax.all_to_all(jnp.broadcast_to(x[None], (count, *x.shape)), axis, 0, 0,...  37.2 us
    all_to_all x2, waiting for transfers between devices, sum_at_owner(): lax.all_to_all(parts, axis, split_axis=0, concat_axis=0, tiled=True)  21.3 us
    all_to_all x3, starting transfers between devices, sent_to_all(): lax.all_to_all(jnp.broadcast_to(x[None], (count, *x.shape)), axis, 0, 0,...  16.7 us
    all_to_all x2, starting transfers between devices, sum_at_owner(): lax.all_to_all(parts, axis, split_axis=0, concat_axis=0, tiled=True)  10.1 us
    dot_general x1, matrix products, per_device(): jnp.dot(code, emit_full, preferred_element_type=jnp.float32)  8.6 us
  transfers between devices with their start and end apart: 7, of which 7 were waited for; matrix products, arithmetic and copies ran while one was open for 9% of the time, Pallas kernels for 0%

commit v1 on v0

v1 whole, which is shorter than its diff:
```python
import jax
import jax.numpy as jnp
from jax import lax
from jax.experimental import pallas as pl
from jax.experimental.pallas import tpu as pltpu
from jax.sharding import PartitionSpec as P

MESH = pl.DeviceIdType.MESH
BF16 = jnp.bfloat16
F32 = jnp.float32

NY, NZH, NX, NZL, NK = 4, 2, 4, 4, 2
NE, NC = NY * NZH, NX * NZL * NK
SLOTS = 8
SAMPLES = 512
CPAD = 128
ROWS = SLOTS * CPAD
HID = 2048
FEAT = 768
CLIENTS = 256
HB = HID // NE
QR = HB // NX


def dot(a, b):
    return jnp.dot(a, b, preferred_element_type=F32)


def dot_nt(a, b):
    return lax.dot_general(a, b, (((1,), (1,)), ((), ())), preferred_element_type=F32)


def dot_tn(a, b):
    return lax.dot_general(a, b, (((0,), (0,)), ((), ())), preferred_element_type=F32)


def sigmoid(v):
    return 0.5 * jnp.tanh(0.5 * v) + 0.5


def step_kernel(
    feats_hbm, labels_ref, ids_ref, trunk_hbm, tw_hbm, table_hbm, emit_hbm,
    loss_ref, egrad_ref, tgrad_ref,
    feats, trunk, tw, table, tablef, wfull,
    pre_send, pre_recv, pre_own, spre, dpre,
    code, code_t, dcode, heads, probs, tops,
    st_send, st_recv, res_send, res_recv,
    gh, eg, egr, am, rx, ry, bx, rxy, by, ryx, cz, rz,
    gs_send, gs_recv, gp_send, gp_recv, trunk_perm,
    loc_sem, pre_ssem, pre_rsem,
    wa_s, wa_r, wz_s, wz_r, wb_s, wb_r, wc_s, wc_r, wd_s, wd_r,
    st_s, st_r, res_s, res_r, core_s, core_r,
    x1_s, x1_r, y1_s, y1_r, x2_s, x2_r, y2_s, y2_r, z_s, z_r,
    gs_s, gs_r, gp_ssem, gp_rsem,
):
    e = lax.axis_index("emit")
    c = lax.axis_index("client")
    y, zh = e // NZH, e % NZH
    x, zl, core = c // (NZL * NK), (c // NK) % NZL, c % NK
    z = zh * NZL + zl
    classes = table_hbm.shape[0]

    def dev(y_=None, z_=None, x_=None, core_=None):
        y_ = y if y_ is None else y_
        z_ = z if z_ is None else z_
        x_ = x if x_ is None else x_
        core_ = core if core_ is None else core_
        return {"emit": y_ * NZH + z_ // NZL, "client": (x_ * NZL + z_ % NZL) * NK + core_}

    def remote(src, dst, ssem, rsem, to):
        return pltpu.make_async_remote_copy(
            src_ref=src, dst_ref=dst, send_sem=ssem, recv_sem=rsem, device_id=to, device_id_type=MESH
        )

    own_w = wfull.at[y, zh]
    ld_trunk = pltpu.make_async_copy(trunk_hbm, trunk, loc_sem.at[0])
    ld_tw = pltpu.make_async_copy(tw_hbm, tw, loc_sem.at[1])
    ld_w = pltpu.make_async_copy(emit_hbm, own_w, loc_sem.at[2])
    ld_table = pltpu.make_async_copy(table_hbm, table, loc_sem.at[3])
    ld_feats = pltpu.make_async_copy(feats_hbm, feats, loc_sem.at[4])
    for cp in (ld_w, ld_trunk, ld_tw, ld_table, ld_feats):
        cp.start()

    ld_w.wait()
    qrow = x * QR + core * (QR // NK)
    qpart = pl.ds(pl.multiple_of(qrow, QR // NK), QR // NK)
    hpart = pl.ds(pl.multiple_of(core * (HB // NK), HB // NK), HB // NK)
    w_z = remote(wfull.at[y, zh, qpart], wfull.at[y, zh, qpart], wz_s, wz_r, dev(z_=2 * NZL - 1 - z))
    w_z.start()
    w_a = []
    for d in range(1, NY):
        part = wfull.at[y, zh, hpart]
        cp = remote(part, part, wa_s.at[d - 1], wa_r.at[d - 1], dev(y_=(y + d) % NY))
        cp.start()
        w_a.append(cp)

    ld_trunk.wait()
    ld_tw.wait()
    cols = dot_nt(trunk[...], tw[...]).astype(BF16)
    width = cols.shape[1]
    spread = (
        lax.broadcasted_iota(jnp.int32, (width, NK * width), 1)
        == lax.broadcasted_iota(jnp.int32, (width, NK * width), 0) + core * width
    ).astype(BF16)
    cols = dot(cols, spread).astype(BF16)
    picker = (
        lax.broadcasted_iota(jnp.int32, (CLIENTS, CLIENTS), 0) == ids_ref[...]
    ).astype(BF16)
    pre_send[...] = dot_tn(picker, cols).reshape(NC, SLOTS, NK * width)

    def send_pre(d, carry):
        to = (c + d) % NC
        remote(pre_send.at[to], pre_recv.at[c], pre_ssem, pre_rsem, {"client": to}).start()
        return carry

    lax.fori_loop(1, NC, send_pre, 0)
    own_pre = pltpu.make_async_copy(pre_send.at[c], pre_recv.at[c], pre_rsem)
    own_pre.start()

    w_z.wait()
    w_b = []
    for d in range(1, NY):
        part = wfull.at[y, 1 - zh, qpart]
        cp = remote(part, part, wb_s.at[d - 1], wb_r.at[d - 1], dev(y_=(y + d) % NY))
        cp.start()
        w_b.append(cp)

    trunk_perm[...] = dot_tn(picker, trunk[...]).astype(BF16)
    ld_table.wait()
    tablef[...] = jnp.zeros_like(tablef)
    tablef[0:classes, :] = table[...].astype(F32)

    for cp in w_b:
        cp.wait()
    w_c = []
    for d in range(1, NX):
        part = wfull.at[:, 1 - zh, qpart]
        cp = remote(part, part, wc_s.at[d - 1], wc_r.at[d - 1], dev(x_=(x + d) % NX))
        cp.start()
        w_c.append(cp)

    pltpu.make_async_copy(pre_recv, pre_recv, pre_rsem).wait()
    for j in range(HID // CPAD):
        pre_own[:, j * CPAD : (j + 1) * CPAD] = pre_recv[NK * j] + pre_recv[NK * j + 1]
    pre = pre_own[...]
    sig = sigmoid(pre)
    spre[...] = pre * sig
    dp = sig * (1.0 + pre * (1.0 - sig))
    for j in range(NE):
        dpre[j] = dp[:, j * HB : (j + 1) * HB]

    live = lax.broadcasted_iota(jnp.int32, (CPAD, HB), 0) < classes

    def emit_codes(first, last):
        def one(i, carry):
            s, h = i // NE, i % NE
            lanes = pl.ds(pl.multiple_of(h * HB, HB), HB)
            rows = pl.ds(pl.multiple_of(s * CPAD, CPAD), CPAD)
            v = spre[pl.ds(s, 1), lanes] + tablef[:, lanes]
            g = sigmoid(v)
            a = v * g
            code[rows, lanes] = jnp.where(live, a, 0.0).astype(BF16)
            dcode[rows, lanes] = (g + a * (1.0 - g)).astype(BF16)
            return carry

        lax.fori_loop(first * NE, last * NE, one, 0)

    emit_codes(0, 4)
    w_d = []
    for i, cp in enumerate(w_a):
        cp.wait()
        part = wfull.at[(y + NY - 1 - i) % NY, zh, hpart]
        cp = remote(part, part, wd_s.at[i], wd_r.at[i], dev(core_=1 - core))
        cp.start()
        w_d.append(cp)
    emit_codes(4, 8)
    for cp in w_c:
        cp.wait()
    for q in range(NX):
        part = wfull.at[:, 1 - zh, pl.ds(pl.multiple_of(q * QR + core * (QR // NK), QR // NK), QR // NK)]
        cp = remote(part, part, wd_s.at[3 + q], wd_r.at[3 + q], dev(core_=1 - core))
        cp.start()
        w_d.append(cp)
    for cp in w_d:
        cp.wait()

    def make_heads(m, carry):
        rows = pl.ds(pl.multiple_of(m * HB, HB), HB)
        heads[rows, :] = dot(code[rows, :], wfull[...].reshape(HID, FEAT)).astype(BF16)
        return carry

    lax.fori_loop(0, ROWS // HB, make_heads, 0)
    ld_feats.wait()

    kids = lax.broadcasted_iota(jnp.int32, (CPAD, SAMPLES), 0)
    valid = kids < classes
    kids = kids + e * classes

    def onehot_of(s):
        return jnp.logical_and(kids == labels_ref[pl.ds(s, 1), :], valid)

    def logits_of(s, carry):
        rows = pl.ds(pl.multiple_of(s * CPAD, CPAD), CPAD)
        frows = pl.ds(pl.multiple_of(s * SAMPLES, SAMPLES), SAMPLES)
        lg = dot_nt(heads[rows, :], feats[frows, :])
        top = jnp.max(jnp.where(valid, lg, -jnp.inf), axis=0, keepdims=True)
        ex = jnp.where(valid, jnp.exp(lg - top), 0.0)
        probs[rows, :] = ex
        tops[pl.ds(s, 1), :] = top
        st_send[s, 0:1, :] = top
        st_send[s, 1:2, :] = jnp.sum(ex, axis=0, keepdims=True)
        st_send[s, 2:3, :] = jnp.sum(jnp.where(onehot_of(s), lg, 0.0), axis=0, keepdims=True)
        st_send[s, 3:4, :] = top
        return carry

    lax.fori_loop(0, SLOTS, logits_of, 0)

    st = []
    for d in range(1, NE):
        to = (e + d) % NE
        cp = remote(st_send.at[to], st_recv.at[d - 1], st_s.at[d - 1], st_r.at[d - 1], {"emit": to})
        cp.start()
        st.append(cp)

    def turn(i, carry):
        s, h = i // NE, i % NE
        rows = pl.ds(pl.multiple_of(s * CPAD, CPAD), CPAD)
        lanes = pl.ds(pl.multiple_of(h * HB, HB), HB)
        code_t[h, :, rows] = code[rows, lanes].T
        return carry

    lax.fori_loop(0, SLOTS * NE // 2, turn, 0)

    for cp in st:
        cp.wait()
    own_st = st_send[e]
    every = [own_st] + [st_recv[d] for d in range(NE - 1)]
    gtop = every[0][0:1]
    for it in every[1:]:
        gtop = jnp.maximum(gtop, it[0:1])
    total = jnp.zeros_like(gtop)
    target = jnp.zeros_like(gtop)
    for it in every:
        total += it[1:2] * jnp.exp(it[0:1] - gtop)
        target += it[2:3]
    logz = gtop + jnp.log(total)
    res_send[0:1, :] = logz
    res_send[1:2, :] = logz - target
    rs = []
    for d in range(1, NE):
        cp = remote(res_send, res_recv.at[e], res_s.at[d - 1], res_r.at[d - 1], {"emit": (e + d) % NE})
        cp.start()
        rs.append(cp)
    res_recv[e] = res_send[...]
    lax.fori_loop(SLOTS * NE // 2, SLOTS * NE, turn, 0)
    for cp in rs:
        cp.wait()

    def grads_of(s, carry):
        rows = pl.ds(pl.multiple_of(s * CPAD, CPAD), CPAD)
        frows = pl.ds(pl.multiple_of(s * SAMPLES, SAMPLES), SAMPLES)
        scale = jnp.exp(tops[pl.ds(s, 1), :] - res_recv[s, 0:1, :])
        g = probs[rows, :] * scale - onehot_of(s).astype(F32)
        gh[rows, :] = dot((g * (1.0 / CLIENTS)).astype(BF16), feats[frows, :]).astype(BF16)
        loss_ref[pl.ds(s, 1), :] = res_recv[s, 1:2, :]
        return carry

    lax.fori_loop(0, SLOTS, grads_of, 0)

    def core_copy(n):
        return remote(eg.at[n, 1 - core], egr.at[n], core_s.at[n], core_r.at[n], dev(core_=1 - core))

    def x1_copy(i, d):
        to = (x + d) % NX
        part = pl.ds(pl.multiple_of(to * 32, 32), 32)
        return remote(am.at[2 * i, part], rx.at[i, d - 1], x1_s.at[i, d - 1], x1_r.at[i, d - 1], dev(x_=to))

    def y1_copy(i):
        return remote(am.at[2 * i + 1], ry.at[i], y1_s.at[i], y1_r.at[i], dev(y_=(y + 1 + i) % NY))

    def compute_chunk(i):
        yy = (y + 1 + i) % NY
        for half in range(NZH):
            n = 2 * i + half
            part = dot(code_t[yy * NZH + half], gh[...]).reshape(16, NK, 8, FEAT)
            for k in range(NK):
                eg[n, k] = part[:, k].reshape(HB // NK, FEAT).astype(BF16)
            core_copy(n).start()

    def pass_on(i, last):
        for half in range(NZH):
            n = 2 * i + half
            core_copy(n).wait()
            am[n] = (eg[n, core].astype(F32) + egr[n].astype(F32)).astype(BF16)
            if half == 0:
                for d in range(1, NX):
                    x1_copy(i, d).start()
            elif not last:
                y1_copy(i).start()

    compute_chunk(0)

    def chunk_step(i, carry):
        compute_chunk(i)
        pass_on(i - 1, False)
        return carry

    lax.fori_loop(1, NY, chunk_step, 0)

    def sum_codes(h, carry):
        gc = dot_nt(gh[...], wfull[h // NZH, h % NZH])
        for s in range(SLOTS):
            lanes = pl.ds(pl.multiple_of(h * HB, HB), HB)
            part = gc[s * CPAD : (s + 1) * CPAD] * dcode[s * CPAD : (s + 1) * CPAD, lanes].astype(F32)
            gs_send[h, s : s + 1, :] = jnp.sum(part, axis=0, keepdims=True)
        return carry

    lax.fori_loop(0, 1, sum_codes, 0)
    pass_on(NY - 1, True)
    lax.fori_loop(1, NE, sum_codes, 0)

    gs = []
    for d in range(1, NE):
        to = (e + d) % NE
        cp = remote(gs_send.at[to], gs_recv.at[d - 1], gs_s.at[d - 1], gs_r.at[d - 1], {"emit": to})
        cp.start()
        gs.append(cp)

    xpart = pl.ds(pl.multiple_of(x * 32, 32), 32)
    y2 = []
    for i in range(NY):
        for d in range(1, NX):
            x1_copy(i, d).wait()
        acc = am[2 * i, xpart, :].astype(F32)
        for d in range(NX - 1):
            acc += rx[i, d].astype(F32)
        bx[i] = acc.astype(BF16)
        if i < NY - 1:
            cp = remote(bx.at[i], rxy.at[i], y2_s.at[i], y2_r.at[i], dev(y_=(y + 1 + i) % NY))
            cp.start()
            y2.append(cp)
    acc = am[2 * NY - 1].astype(F32)
    for i in range(NY - 1):
        y1_copy(i).wait()
        acc += ry[i].astype(F32)
    by[...] = acc.astype(BF16)
    x2 = []
    for d in range(1, NX):
        to = (x + d) % NX
        part = pl.ds(pl.multiple_of(to * 32, 32), 32)
        cp = remote(by.at[part], ryx.at[d - 1], x2_s.at[d - 1], x2_r.at[d - 1], dev(x_=to))
        cp.start()
        x2.append(cp)

    for cp in gs:
        cp.wait()
    block = gs_send[e]
    for d in range(NE - 1):
        block = block + gs_recv[d]
    gp_send[...] = (block * dpre[e]).astype(BF16)

    def send_gp(d, carry):
        remote(gp_send, gp_recv.at[c], gp_ssem, gp_rsem, {"client": (c + d) % NC}).start()
        return carry

    lax.fori_loop(1, NC, send_gp, 0)
    own_gp = pltpu.make_async_copy(gp_send, gp_recv.at[c], gp_rsem)
    own_gp.start()

    for cp in y2:
        cp.wait()
    acc = bx[NY - 1].astype(F32)
    for d in range(NY - 1):
        acc += rxy[d].astype(F32)
    cz[0:NZL] = acc.astype(BF16).reshape(NZL, 8, FEAT)
    for cp in x2:
        cp.wait()
    acc = by[xpart, :].astype(F32)
    for d in range(NX - 1):
        acc += ryx[d].astype(F32)
    cz[NZL:] = acc.astype(BF16).reshape(NZL, 8, FEAT)
    nz = NZH * NZL
    zs = []
    for d in range(1, nz):
        to = (z + d) % nz
        cp = remote(cz.at[to], rz.at[d - 1], z_s.at[d - 1], z_r.at[d - 1], dev(z_=to))
        cp.start()
        zs.append(cp)

    pltpu.make_async_copy(gp_recv, gp_recv, gp_rsem).wait()
    select = (
        lax.broadcasted_iota(jnp.int32, (8, HB), 1) == lax.broadcasted_iota(jnp.int32, (8, HB), 0) + c * 8
    ).astype(BF16)
    mine = dot_nt(select, gp_recv[...].reshape(CLIENTS, HB)).astype(BF16)
    tgrad_ref[...] = dot(mine, trunk_perm[...])

    for cp in zs:
        cp.wait()
    acc = cz[z].astype(F32)
    for d in range(nz - 1):
        acc += rz[d].astype(F32)
    egrad_ref[...] = acc

    remote(pre_send.at[0 : NC - 1], pre_recv.at[0 : NC - 1], pre_ssem, pre_rsem, {"client": (c + 1) % NC}).wait_send()
    remote(gp_recv.at[0 : NC - 1], gp_recv.at[0 : NC - 1], gp_ssem, gp_rsem, {"client": (c + 1) % NC}).wait_send()


def per_device(features, labels, client_ids, trunk_in, trunk_weight, class_table, emit_weight):
    vm = pltpu.VMEM
    dma = pltpu.SemaphoreType.DMA
    half = HB // NK
    scratch = [
        vm((SLOTS * SAMPLES, FEAT), BF16), vm((CLIENTS, HID), BF16), vm((trunk_weight.shape[1], HID), BF16),
        vm(class_table.shape, BF16), vm((CPAD, HID), F32), vm((NY, NZH, HB, FEAT), BF16),
        vm((NC, SLOTS, CPAD), F32), vm((NC, SLOTS, CPAD), F32), vm((SLOTS, HID), F32), vm((SLOTS, HID), F32),
        vm((NE, SLOTS, HB), F32),
        vm((ROWS, HID), BF16), vm((NE, HB, ROWS), BF16), vm((ROWS, HID), BF16), vm((ROWS, FEAT), BF16),
        vm((ROWS, SAMPLES), F32), vm((SLOTS, SAMPLES), F32),
        vm((SLOTS, 4, SAMPLES), F32), vm((NE - 1, 4, SAMPLES), F32), vm((2, SAMPLES), F32), vm((SLOTS, 2, SAMPLES), F32),
        vm((ROWS, FEAT), BF16), vm((NE, NK, half, FEAT), BF16), vm((NE, half, FEAT), BF16), vm((NE, half, FEAT), BF16),
        vm((NY, NX - 1, 32, FEAT), BF16), vm((NY - 1, half, FEAT), BF16),
        vm((NY, 32, FEAT), BF16), vm((NY - 1, 32, FEAT), BF16), vm((half, FEAT), BF16), vm((NX - 1, 32, FEAT), BF16),
        vm((NZH * NZL, 8, FEAT), BF16), vm((NZH * NZL - 1, 8, FEAT), BF16),
        vm((NE, SLOTS, HB), F32), vm((NE - 1, SLOTS, HB), F32), vm((SLOTS, HB), BF16), vm((NC, SLOTS, HB), BF16),
        vm((CLIENTS, HID), BF16),
        dma((5,)), dma, dma,
        dma((3,)), dma((3,)), dma, dma, dma((3,)), dma((3,)), dma((3,)), dma((3,)), dma((7,)), dma((7,)),
        dma((7,)), dma((7,)), dma((7,)), dma((7,)), dma((8,)), dma((8,)),
        dma((4, 3)), dma((4, 3)), dma((3,)), dma((3,)), dma((3,)), dma((3,)), dma((3,)), dma((3,)), dma((7,)), dma((7,)),
        dma((7,)), dma((7,)), dma, dma,
    ]
    hbm = pl.BlockSpec(memory_space=pl.ANY)
    here = pl.BlockSpec(memory_space=pltpu.VMEM)
    loss, egrad, tgrad = pl.pallas_call(
        step_kernel,
        name="hyper_step",
        out_shape=(
            jax.ShapeDtypeStruct((SLOTS, SAMPLES), F32),
            jax.ShapeDtypeStruct((HID // (NE * NC), FEAT), F32),
            jax.ShapeDtypeStruct((HID // (NE * NC), HID), F32),
        ),
        in_specs=[hbm, here, here, hbm, hbm, hbm, hbm],
        out_specs=(here, here, here),
        scratch_shapes=scratch,
        compiler_params=pltpu.CompilerParams(has_side_effects=True, vmem_limit_bytes=56 << 20),
    )(
        features, labels.reshape(SLOTS, SAMPLES), client_ids.reshape(1, CLIENTS), trunk_in, trunk_weight.T,
        class_table, emit_weight,
    )
    return loss.reshape(SLOTS * SAMPLES), egrad, tgrad.T


def solution(mesh):
    return jax.shard_map(
        per_device,
        mesh=mesh,
        in_specs=(
            P("client", None),
            P("client"),
            P(),
            P(),
            P(None, "client"),
            P("emit", None),
            P("emit", None),
        ),
        out_specs=(P("client"), P(("emit", "client"), None), P(None, ("emit", "client"))),
        check_vma=False,
    )
```

time: 303 us -> 102 us (0.34)
  waiting for transfers between devices: 168 us -> 0 us
  Pallas kernels: 0 us -> 94.3 us
  blocking collectives: 37.2 us -> 0 us
  matrix products: 34.9 us -> 0 us
  starting transfers between devices: 27 us -> 0 us
  between operations: 14.3 us -> 0.64 us
  local copies, waits for them, and re-layouts: 14.3 us -> 5.47 us
  other arithmetic: 6.74 us -> 0 us
    pallas_call x0 -> x1, Pallas kernels: none -> 94.3 us  [per_device(): pl.pallas_call(step_kernel, name='hyper_step', out_shape=(jax.ShapeDtypeS...]
    all_to_all x5 -> x0, waiting for transfers between devices: 75 us -> none  [the longest x3 53.7 us: sent_to_all(): lax.all_to_all(jnp.broadcast_to(x[None], (count, *x.shape)), axis, 0, 0,...]
    reduce_scatter x1 -> x0, waiting for transfers between devices: 50.2 us -> none  [per_device(): lax.psum_scatter(jnp.einsum('rh,rd->hd', code, grad_heads, preferred_elem...]
    all_gather x1 -> x0, waiting for transfers between devices: 41.8 us -> none  [per_device(): emit_full = lax.all_gather(emit_weight, 'emit', axis=0, tiled=True)]
    all_to_all x2 -> x0, blocking collectives: 37.2 us -> none  [sent_to_all(): lax.all_to_all(jnp.broadcast_to(x[None], (count, *x.shape)), axis, 0, 0,...]
    dot_general x8 -> x0, matrix products: 34.9 us -> none  [the longest x1 8.6 us: per_device(): jnp.dot(code, emit_full, preferred_element_type=jnp.float32)]
    all_to_all x5 -> x0, starting transfers between devices: 26.9 us -> none  [the longest x3 16.7 us: sent_to_all(): lax.all_to_all(jnp.broadcast_to(x[None], (count, *x.shape)), axis, 0, 0,...]
    add x1 -> x0, local copies, waits for them, and re-layouts: 7.94 us -> none  [per_device(): jax.nn.silu(pre_own)[:, None, :]]
  transfers between devices with their start and end apart: 7 -> 0, of which waited for: 7 -> 0; matrix products, arithmetic and copies ran while one was open for 9% -> 0% of each run, Pallas kernels for 0% -> 0%
where the time goes in v1:
time: 102 us; the launch traced here: 100 us
  Pallas kernels  94.3 us (92%)
  local copies, waits for them, and re-layouts  5.47 us (5%)
    pallas_call x1, Pallas kernels, per_device(): pl.pallas_call(step_kernel, name='hyper_step', out_shape=(jax.ShapeDtypeS...  94.3 us
    unnamed x3, local copies, waits for them, and re-layouts  4.15 us

profile of v1, /device:TPU:1, one launch (start us, length us, event | category | flops | bytes accessed | tf_op | source)
XLA Modules:
  0.0 100.4 jit_solution(10315491170339676018)
XLA Ops:
  0.6 1.3 %reshape.15.labels_ref = s32[8,512]{1,0:T(8,128)} reshape(s32[4096]{0:T(1024)} %param.8) | data formatting | bytes 32768 | tf_op jit(solution)/shard_map/reshape | solution.py:447
  2.0 94.3 %hyper_step.1 = (f32[8,512]{1,0:T(8,128)}, f32[8,768]{1,0:T(8,128)}, f32[8,2048]{1,0:T(8,128)}) custom-call(bf16[4096,768]{1,0:T(8,128)(2,1)} %feats_hbm.1, s32[8,512]{1,0:T(8,128)} %reshape.15.labels_ref, s32[1,256]{1,0:T(1,128)} %bitcast.9, bf16[256,2048]{1,0:T(8,128)(2,1)} %trunk_hbm.1, bf16[64,2048]{1,0:T(8,128)(2,1)} %bitcast.5, ...), custom_call_target="tpu_custom_call" | custom-call | tf_op jit(solution)/shard_map/hyper_step/pallas_call | solution.py:434
  96.2 1.3 %copy.10 = f32[1,4,8,128]{3,1,2,0:T(4,128)} copy(f32[1,4,8,128]{3,2,1,0:T(8,128)} %bitcast.8) | data formatting | bytes 32768
  97.6 1.3 %copy.13 = f32[8,768]{1,0:T(8,128)} copy(f32[8,768]{1,0:T(8,128)} %get-tuple-element.13) | data formatting | bytes 49152
  98.9 1.5 %copy.14 = f32[2048,8]{0,1:T(8,128)} copy(f32[2048,8]{0,1:T(8,128)} %bitcast.6) | data formatting | bytes 131072

commit v2 on v1

--- a/solution.py
+++ b/solution.py
@@ -41,9 +41,9 @@
 def step_kernel(
     feats_hbm, labels_ref, ids_ref, trunk_hbm, tw_hbm, table_hbm, emit_hbm,
     loss_ref, egrad_ref, tgrad_ref,
-    feats, trunk, tw, table, tablef, wfull,
+    feats, lab, trunk, tw, table, tablef, wfull,
     pre_send, pre_recv, pre_own, spre, dpre,
-    code, code_t, dcode, heads, probs, tops,
+    code, code_t, dcode, hacc, heads, probs, tops,
     st_send, st_recv, res_send, res_recv,
     gh, eg, egr, am, rx, ry, bx, rxy, by, ryx, cz, rz,
     gs_send, gs_recv, gp_send, gp_recv, trunk_perm,
@@ -72,27 +72,28 @@
             src_ref=src, dst_ref=dst, send_sem=ssem, recv_sem=rsem, device_id=to, device_id_type=MESH
         )
 
-    own_w = wfull.at[y, zh]
+    barrier = pltpu.get_barrier_semaphore()
+
+    def greet(to):
+        pl.semaphore_signal(barrier, inc=1, device_id=to, device_id_type=MESH)
+
+    def greet_client(d, carry):
+        greet({"client": (c + d) % NC})
+        return carry
+
+    for d in range(1, NE):
+        greet({"emit": (e + d) % NE})
+    for d in range(1, NZL):
+        greet(dev(z_=(1 - zh) * NZL + (zl + d) % NZL))
+    lax.fori_loop(1, NC, greet_client, 0)
+
     ld_trunk = pltpu.make_async_copy(trunk_hbm, trunk, loc_sem.at[0])
     ld_tw = pltpu.make_async_copy(tw_hbm, tw, loc_sem.at[1])
-    ld_w = pltpu.make_async_copy(emit_hbm, own_w, loc_sem.at[2])
+    ld_w = pltpu.make_async_copy(emit_hbm, wfull.at[zh, y], loc_sem.at[2])
     ld_table = pltpu.make_async_copy(table_hbm, table, loc_sem.at[3])
     ld_feats = pltpu.make_async_copy(feats_hbm, feats, loc_sem.at[4])
-    for cp in (ld_w, ld_trunk, ld_tw, ld_table, ld_feats):
-        cp.start()
-
-    ld_w.wait()
-    qrow = x * QR + core * (QR // NK)
-    qpart = pl.ds(pl.multiple_of(qrow, QR // NK), QR // NK)
-    hpart = pl.ds(pl.multiple_of(core * (HB // NK), HB // NK), HB // NK)
-    w_z = remote(wfull.at[y, zh, qpart], wfull.at[y, zh, qpart], wz_s, wz_r, dev(z_=2 * NZL - 1 - z))
-    w_z.start()
-    w_a = []
-    for d in range(1, NY):
-        part = wfull.at[y, zh, hpart]
-        cp = remote(part, part, wa_s.at[d - 1], wa_r.at[d - 1], dev(y_=(y + d) % NY))
-        cp.start()
-        w_a.append(cp)
+    for cp in (ld_trunk, ld_tw, ld_w, ld_table, ld_feats):
+        cp.start()
 
     ld_trunk.wait()
     ld_tw.wait()
@@ -107,6 +108,26 @@
         lax.broadcasted_iota(jnp.int32, (CLIENTS, CLIENTS), 0) == ids_ref[...]
     ).astype(BF16)
     pre_send[...] = dot_tn(picker, cols).reshape(NC, SLOTS, NK * width)
+    ld_table.wait()
+    tablef[...] = jnp.zeros_like(tablef)
+    tablef[0:classes, :] = table[...].astype(F32)
+    for s in range(SLOTS):
+        for j in range(SAMPLES // 128):
+            lab[s : s + 1, j * 128 : (j + 1) * 128] = labels_ref[s * 4 + j : s * 4 + j + 1, :]
+    ld_w.wait()
+
+    pl.semaphore_wait(barrier, NE - 1 + NZL - 1 + NC - 1)
+
+    qrow = x * QR + core * (QR // NK)
+    qpart = pl.ds(pl.multiple_of(qrow, QR // NK), QR // NK)
+    half = HB // NK
+    cut = 32
+
+    def hpart(first, last):
+        return pl.ds(pl.multiple_of(core * half + first, cut), last - first)
+
+    w_z = remote(wfull.at[zh, y, qpart], wfull.at[zh, y, qpart], wz_s, wz_r, dev(z_=2 * NZL - 1 - z))
+    w_z.start()
 
     def send_pre(d, carry):
         to = (c + d) % NC
@@ -116,28 +137,25 @@
     lax.fori_loop(1, NC, send_pre, 0)
     own_pre = pltpu.make_async_copy(pre_send.at[c], pre_recv.at[c], pre_rsem)
     own_pre.start()
+    w_a = []
+    for d in range(1, NY):
+        part = wfull.at[zh, y, hpart(0, cut)]
+        cp = remote(part, part, wa_s.at[0, d - 1], wa_r.at[0, d - 1], dev(y_=(y + d) % NY))
+        cp.start()
+        w_a.append(cp)
 
     w_z.wait()
     w_b = []
     for d in range(1, NY):
-        part = wfull.at[y, 1 - zh, qpart]
+        part = wfull.at[1 - zh, y, qpart]
         cp = remote(part, part, wb_s.at[d - 1], wb_r.at[d - 1], dev(y_=(y + d) % NY))
         cp.start()
         w_b.append(cp)
-
-    trunk_perm[...] = dot_tn(picker, trunk[...]).astype(BF16)
-    ld_table.wait()
-    tablef[...] = jnp.zeros_like(tablef)
-    tablef[0:classes, :] = table[...].astype(F32)
-
-    for cp in w_b:
-        cp.wait()
-    w_c = []
-    for d in range(1, NX):
-        part = wfull.at[:, 1 - zh, qpart]
-        cp = remote(part, part, wc_s.at[d - 1], wc_r.at[d - 1], dev(x_=(x + d) % NX))
-        cp.start()
-        w_c.append(cp)
+    for d in range(1, NY):
+        part = wfull.at[zh, y, hpart(cut, half)]
+        cp = remote(part, part, wa_s.at[1, d - 1], wa_r.at[1, d - 1], dev(y_=(y + d) % NY))
+        cp.start()
+        w_a.append(cp)
 
     pltpu.make_async_copy(pre_recv, pre_recv, pre_rsem).wait()
     for j in range(HID // CPAD):
@@ -151,45 +169,81 @@
 
     live = lax.broadcasted_iota(jnp.int32, (CPAD, HB), 0) < classes
 
-    def emit_codes(first, last):
-        def one(i, carry):
-            s, h = i // NE, i % NE
-            lanes = pl.ds(pl.multiple_of(h * HB, HB), HB)
-            rows = pl.ds(pl.multiple_of(s * CPAD, CPAD), CPAD)
-            v = spre[pl.ds(s, 1), lanes] + tablef[:, lanes]
-            g = sigmoid(v)
-            a = v * g
-            code[rows, lanes] = jnp.where(live, a, 0.0).astype(BF16)
-            dcode[rows, lanes] = (g + a * (1.0 - g)).astype(BF16)
-            return carry
-
-        lax.fori_loop(first * NE, last * NE, one, 0)
-
-    emit_codes(0, 4)
-    w_d = []
-    for i, cp in enumerate(w_a):
-        cp.wait()
-        part = wfull.at[(y + NY - 1 - i) % NY, zh, hpart]
-        cp = remote(part, part, wd_s.at[i], wd_r.at[i], dev(core_=1 - core))
-        cp.start()
-        w_d.append(cp)
-    emit_codes(4, 8)
-    for cp in w_c:
-        cp.wait()
-    for q in range(NX):
-        part = wfull.at[:, 1 - zh, pl.ds(pl.multiple_of(q * QR + core * (QR // NK), QR // NK), QR // NK)]
-        cp = remote(part, part, wd_s.at[3 + q], wd_r.at[3 + q], dev(core_=1 - core))
+    def emit_codes(i, carry):
+        s, h = i // NE, i % NE
+        lanes = pl.ds(pl.multiple_of(h * HB, HB), HB)
+        within = pl.ds(pl.multiple_of((h // NZH) * HB, HB), HB)
+        rows = pl.ds(pl.multiple_of(s * CPAD, CPAD), CPAD)
+        v = spre[pl.ds(s, 1), lanes] + tablef[:, lanes]
+        g = sigmoid(v)
+        a = v * g
+        code[h % NZH, rows, within] = jnp.where(live, a, 0.0).astype(BF16)
+        dcode[rows, lanes] = (g + a * (1.0 - g)).astype(BF16)
+        return carry
+
+    def turn(i, carry):
+        s, h = i // NE, i % NE
+        rows = pl.ds(pl.multiple_of(s * CPAD, CPAD), CPAD)
+        within = pl.ds(pl.multiple_of((h // NZH) * HB, HB), HB)
+        code_t[h, :, rows] = code[h % NZH, rows, within].T
+        return carry
+
+    lax.fori_loop(0, NE, emit_codes, 0)
+
+    for cp in w_b:
+        cp.wait()
+    w_c = []
+    for d in range(1, NX):
+        part = wfull.at[1 - zh, :, qpart]
+        cp = remote(part, part, wc_s.at[d - 1], wc_r.at[d - 1], dev(x_=(x + d) % NX))
+        cp.start()
+        w_c.append(cp)
+
+    def to_core(i, q):
+        part = wfull.at[1 - zh, :, pl.ds(pl.multiple_of(q * QR + core * (QR // NK), QR // NK), QR // NK)]
+        return remote(part, part, wd_s.at[i], wd_r.at[i], dev(core_=1 - core))
+
+    w_d = [to_core(3, x)]
+    w_d[0].start()
+
+    lax.fori_loop(NE, SLOTS * NE, emit_codes, 0)
+    lax.fori_loop(0, SLOTS * NE // 2, turn, 0)
+    trunk_perm[...] = dot_tn(picker, trunk[...]).astype(BF16)
+
+    w_e = []
+    for d in range(1, NY):
+        w_a[d - 1].wait()
+        w_a[NY - 1 + d - 1].wait()
+        part = wfull.at[zh, (y + NY - d) % NY, hpart(0, half)]
+        cp = remote(part, part, wd_s.at[d - 1], wd_r.at[d - 1], dev(core_=1 - core))
+        cp.start()
+        w_e.append(cp)
+    lax.fori_loop(SLOTS * NE // 2, SLOTS * NE, turn, 0)
+    for cp in w_e:
+        cp.wait()
+
+    def heads_first(m, carry):
+        rows = pl.ds(pl.multiple_of(m * HB, HB), HB)
+        hacc[rows, :] = dot(code[zh, rows, :], wfull[zh].reshape(HID // NZH, FEAT))
+        return carry
+
+    lax.fori_loop(0, ROWS // HB, heads_first, 0)
+
+    for d in range(1, NX):
+        w_c[d - 1].wait()
+        cp = to_core(3 + d, (x + NX - d) % NX)
         cp.start()
         w_d.append(cp)
     for cp in w_d:
         cp.wait()
 
-    def make_heads(m, carry):
+    def heads_rest(m, carry):
         rows = pl.ds(pl.multiple_of(m * HB, HB), HB)
-        heads[rows, :] = dot(code[rows, :], wfull[...].reshape(HID, FEAT)).astype(BF16)
-        return carry
-
-    lax.fori_loop(0, ROWS // HB, make_heads, 0)
+        part = dot(code[1 - zh, rows, :], wfull[1 - zh].reshape(HID // NZH, FEAT))
+        heads[rows, :] = (hacc[rows, :] + part).astype(BF16)
+        return carry
+
+    lax.fori_loop(0, ROWS // HB, heads_rest, 0)
     ld_feats.wait()
 
     kids = lax.broadcasted_iota(jnp.int32, (CPAD, SAMPLES), 0)
@@ -197,7 +251,7 @@
     kids = kids + e * classes
 
     def onehot_of(s):
-        return jnp.logical_and(kids == labels_ref[pl.ds(s, 1), :], valid)
+        return jnp.logical_and(kids == lab[pl.ds(s, 1), :], valid)
 
     def logits_of(s, carry):
         rows = pl.ds(pl.multiple_of(s * CPAD, CPAD), CPAD)
@@ -221,15 +275,6 @@
         cp = remote(st_send.at[to], st_recv.at[d - 1], st_s.at[d - 1], st_r.at[d - 1], {"emit": to})
         cp.start()
         st.append(cp)
-
-    def turn(i, carry):
-        s, h = i // NE, i % NE
-        rows = pl.ds(pl.multiple_of(s * CPAD, CPAD), CPAD)
-        lanes = pl.ds(pl.multiple_of(h * HB, HB), HB)
-        code_t[h, :, rows] = code[rows, lanes].T
-        return carry
-
-    lax.fori_loop(0, SLOTS * NE // 2, turn, 0)
 
     for cp in st:
         cp.wait()
@@ -252,7 +297,6 @@
         cp.start()
         rs.append(cp)
     res_recv[e] = res_send[...]
-    lax.fori_loop(SLOTS * NE // 2, SLOTS * NE, turn, 0)
     for cp in rs:
         cp.wait()
 
@@ -262,10 +306,13 @@
         scale = jnp.exp(tops[pl.ds(s, 1), :] - res_recv[s, 0:1, :])
         g = probs[rows, :] * scale - onehot_of(s).astype(F32)
         gh[rows, :] = dot((g * (1.0 / CLIENTS)).astype(BF16), feats[frows, :]).astype(BF16)
-        loss_ref[pl.ds(s, 1), :] = res_recv[s, 1:2, :]
         return carry
 
     lax.fori_loop(0, SLOTS, grads_of, 0)
+
+    for s in range(SLOTS):
+        for j in range(SAMPLES // 128):
+            loss_ref[s * 4 + j : s * 4 + j + 1, :] = res_recv[s, 1:2, j * 128 : (j + 1) * 128]
 
     def core_copy(n):
         return remote(eg.at[n, 1 - core], egr.at[n], core_s.at[n], core_r.at[n], dev(core_=1 - core))
@@ -308,7 +355,7 @@
     lax.fori_loop(1, NY, chunk_step, 0)
 
     def sum_codes(h, carry):
-        gc = dot_nt(gh[...], wfull[h // NZH, h % NZH])
+        gc = dot_nt(gh[...], wfull[h % NZH, h // NZH])
         for s in range(SLOTS):
             lanes = pl.ds(pl.multiple_of(h * HB, HB), HB)
             part = gc[s * CPAD : (s + 1) * CPAD] * dcode[s * CPAD : (s + 1) * CPAD, lanes].astype(F32)
@@ -405,16 +452,23 @@
     remote(gp_recv.at[0 : NC - 1], gp_recv.at[0 : NC - 1], gp_ssem, gp_rsem, {"client": (c + 1) % NC}).wait_send()
 
 
+def hand_over(loss_in, egrad_in, tgrad_in, loss_ref, egrad_ref, tgrad_ref):
+    loss_ref[...] = loss_in[...]
+    egrad_ref[...] = egrad_in[...]
+    tgrad_ref[...] = tgrad_in[...]
+
+
 def per_device(features, labels, client_ids, trunk_in, trunk_weight, class_table, emit_weight):
     vm = pltpu.VMEM
     dma = pltpu.SemaphoreType.DMA
     half = HB // NK
     scratch = [
-        vm((SLOTS * SAMPLES, FEAT), BF16), vm((CLIENTS, HID), BF16), vm((trunk_weight.shape[1], HID), BF16),
-        vm(class_table.shape, BF16), vm((CPAD, HID), F32), vm((NY, NZH, HB, FEAT), BF16),
+        vm((SLOTS * SAMPLES, FEAT), BF16), vm((SLOTS, SAMPLES), jnp.int32), vm((CLIENTS, HID), BF16), vm((trunk_weight.shape[1], HID), BF16),
+        vm(class_table.shape, BF16), vm((CPAD, HID), F32), vm((NZH, NY, HB, FEAT), BF16),
         vm((NC, SLOTS, CPAD), F32), vm((NC, SLOTS, CPAD), F32), vm((SLOTS, HID), F32), vm((SLOTS, HID), F32),
         vm((NE, SLOTS, HB), F32),
-        vm((ROWS, HID), BF16), vm((NE, HB, ROWS), BF16), vm((ROWS, HID), BF16), vm((ROWS, FEAT), BF16),
+        vm((NZH, ROWS, HID // NZH), BF16), vm((NE, HB, ROWS), BF16), vm((ROWS, HID), BF16), vm((ROWS, FEAT), F32),
+        vm((ROWS, FEAT), BF16),
         vm((ROWS, SAMPLES), F32), vm((SLOTS, SAMPLES), F32),
         vm((SLOTS, 4, SAMPLES), F32), vm((NE - 1, 4, SAMPLES), F32), vm((2, SAMPLES), F32), vm((SLOTS, 2, SAMPLES), F32),
         vm((ROWS, FEAT), BF16), vm((NE, NK, half, FEAT), BF16), vm((NE, half, FEAT), BF16), vm((NE, half, FEAT), BF16),
@@ -424,7 +478,7 @@
         vm((NE, SLOTS, HB), F32), vm((NE - 1, SLOTS, HB), F32), vm((SLOTS, HB), BF16), vm((NC, SLOTS, HB), BF16),
         vm((CLIENTS, HID), BF16),
         dma((5,)), dma, dma,
-        dma((3,)), dma((3,)), dma, dma, dma((3,)), dma((3,)), dma((3,)), dma((3,)), dma((7,)), dma((7,)),
+        dma((2, 3)), dma((2, 3)), dma, dma, dma((3,)), dma((3,)), dma((3,)), dma((3,)), dma((7,)), dma((7,)),
         dma((7,)), dma((7,)), dma((7,)), dma((7,)), dma((8,)), dma((8,)),
         dma((4, 3)), dma((4, 3)), dma((3,)), dma((3,)), dma((3,)), dma((3,)), dma((3,)), dma((3,)), dma((7,)), dma((7,)),
         dma((7,)), dma((7,)), dma, dma,
@@ -435,18 +489,26 @@
         step_kernel,
         name="hyper_step",
         out_shape=(
-            jax.ShapeDtypeStruct((SLOTS, SAMPLES), F32),
+            jax.ShapeDtypeStruct((SLOTS * SAMPLES // 128, 128), F32),
             jax.ShapeDtypeStruct((HID // (NE * NC), FEAT), F32),
             jax.ShapeDtypeStruct((HID // (NE * NC), HID), F32),
         ),
         in_specs=[hbm, here, here, hbm, hbm, hbm, hbm],
         out_specs=(here, here, here),
         scratch_shapes=scratch,
-        compiler_params=pltpu.CompilerParams(has_side_effects=True, vmem_limit_bytes=56 << 20),
+        compiler_params=pltpu.CompilerParams(collective_id=0, has_side_effects=True, vmem_limit_bytes=56 << 20),
     )(
-        features, labels.reshape(SLOTS, SAMPLES), client_ids.reshape(1, CLIENTS), trunk_in, trunk_weight.T,
+        features, labels.reshape(SLOTS * SAMPLES // 128, 128), client_ids.reshape(1, CLIENTS), trunk_in, trunk_weight.T,
         class_table, emit_weight,
     )
+    outs = (loss, egrad, tgrad)
+    loss, egrad, tgrad = pl.pallas_call(
+        hand_over,
+        name="hand_over",
+        out_shape=tuple(jax.ShapeDtypeStruct(o.shape, o.dtype) for o in outs),
+        in_specs=[here] * 3,
+        out_specs=(here,) * 3,
+    )(*outs)
     return loss.reshape(SLOTS * SAMPLES), egrad, tgrad.T
 
 

time: 102 us -> 86.9 us (0.85)
  Pallas kernels: 94.3 us -> 84.6 us
  local copies, waits for them, and re-layouts: 5.47 us -> 0 us
    pallas_call x1, Pallas kernels: 94.3 us -> 83 us  [per_device(): pl.pallas_call(step_kernel, name='hyper_step', out_shape=(jax.ShapeDtypeS...]
    unnamed x3 -> x0, local copies, waits for them, and re-layouts: 4.15 us -> none
    pallas_call x0 -> x1, Pallas kernels: none -> 1.52 us  [per_device(): pl.pallas_call(hand_over, name='hand_over', out_shape=tuple((jax.ShapeDty...]
    reshape x1 -> x0, local copies, waits for them, and re-layouts: 1.33 us -> none  [per_device(): labels.reshape(SLOTS, SAMPLES)]
where the time goes in v2:
time: 86.9 us; the launch traced here: 85.2 us
  Pallas kernels  84.6 us (97%)
    pallas_call x1, Pallas kernels, per_device(): pl.pallas_call(step_kernel, name='hyper_step', out_shape=(jax.ShapeDtypeS...  83 us

profile of v2, /device:TPU:1, one launch (start us, length us, event | category | flops | bytes accessed | tf_op | source)
XLA Modules:
  0.0 85.2 jit_solution(4079741904262002053)
XLA Ops:
  0.6 83.0 %hyper_step.1 = (f32[32,128]{1,0:T(8,128)}, f32[8,768]{1,0:T(8,128)}, f32[8,2048]{1,0:T(8,128)}) custom-call(bf16[4096,768]{1,0:T(8,128)(2,1)} %feats_hbm.1, s32[32,128]{1,0:T(8,128)} %bitcast.6, s32[1,256]{1,0:T(1,128)} %bitcast.7, bf16[256,2048]{1,0:T(8,128)(2,1)} %trunk_hbm.1, bf16[64,2048]{1,0:T(8,128)(2,1)} %bitcast.5, bf16[125,2048]{1,0:T(8,128)(2,1)} %table_hbm.1, ...), custom_call_target="tpu_custom_call" | custom-call | tf_op jit(solution)/shard_map/hyper_step/pallas_call | solution.py:488
  83.7 1.5 %hand_over.1 = (f32[32,128]{1,0:T(8,128)}, f32[8,768]{1,0:T(8,128)}, f32[8,2048]{1,0:T(8,128)}) custom-call(f32[32,128]{1,0:T(8,128)} %get-tuple-element.9.loss_in, f32[8,768]{1,0:T(8,128)} %get-tuple-element.10.egrad_in, f32[8,2048]{1,0:T(8,128)} %get-tuple-element.11.tgrad_in), custom_call_target="tpu_custom_call" | custom-call | tf_op jit(solution)/shard_map/hand_over/pallas_call | solution.py:505

commit v3 on v2

--- a/solution.py
+++ b/solution.py
@@ -44,7 +44,7 @@
     feats, lab, trunk, tw, table, tablef, wfull,
     pre_send, pre_recv, pre_own, spre, dpre,
     code, code_t, dcode, hacc, heads, probs, tops,
-    st_send, st_recv, res_send, res_recv,
+    sums, logz, st_send, st_recv, tg_send, tg_recv,
     gh, eg, egr, am, rx, ry, bx, rxy, by, ryx, cz, rz,
     gs_send, gs_recv, gp_send, gp_recv, trunk_perm,
     loc_sem, pre_ssem, pre_rsem,
@@ -121,7 +121,7 @@
     qrow = x * QR + core * (QR // NK)
     qpart = pl.ds(pl.multiple_of(qrow, QR // NK), QR // NK)
     half = HB // NK
-    cut = 32
+    cut = 64
 
     def hpart(first, last):
         return pl.ds(pl.multiple_of(core * half + first, cut), last - first)
@@ -151,11 +151,17 @@
         cp = remote(part, part, wb_s.at[d - 1], wb_r.at[d - 1], dev(y_=(y + d) % NY))
         cp.start()
         w_b.append(cp)
-    for d in range(1, NY):
-        part = wfull.at[zh, y, hpart(cut, half)]
-        cp = remote(part, part, wa_s.at[1, d - 1], wa_r.at[1, d - 1], dev(y_=(y + d) % NY))
-        cp.start()
-        w_a.append(cp)
+
+    def along_x(i, yy):
+        copies = []
+        for d in range(1, NX):
+            part = wfull.at[1 - zh, yy, qpart]
+            cp = remote(part, part, wc_s.at[i, d - 1], wc_r.at[i, d - 1], dev(x_=(x + d) % NX))
+            cp.start()
+            copies.append(cp)
+        return copies
+
+    w_c = [along_x(0, y)]
 
     pltpu.make_async_copy(pre_recv, pre_recv, pre_rsem).wait()
     for j in range(HID // CPAD):
@@ -188,16 +194,16 @@
         code_t[h, :, rows] = code[h % NZH, rows, within].T
         return carry
 
-    lax.fori_loop(0, NE, emit_codes, 0)
-
-    for cp in w_b:
-        cp.wait()
-    w_c = []
-    for d in range(1, NX):
-        part = wfull.at[1 - zh, :, qpart]
-        cp = remote(part, part, wc_s.at[d - 1], wc_r.at[d - 1], dev(x_=(x + d) % NX))
-        cp.start()
-        w_c.append(cp)
+    lax.fori_loop(0, SLOTS * NE, emit_codes, 0, unroll=2)
+
+    for d in range(1, NY):
+        part = wfull.at[zh, y, hpart(cut, half)]
+        cp = remote(part, part, wa_s.at[1, d - 1], wa_r.at[1, d - 1], dev(y_=(y + d) % NY))
+        cp.start()
+        w_a.append(cp)
+    for d in range(1, NY):
+        w_b[d - 1].wait()
+        w_c.append(along_x(d, (y + NY - d) % NY))
 
     def to_core(i, q):
         part = wfull.at[1 - zh, :, pl.ds(pl.multiple_of(q * QR + core * (QR // NK), QR // NK), QR // NK)]
@@ -206,7 +212,6 @@
     w_d = [to_core(3, x)]
     w_d[0].start()
 
-    lax.fori_loop(NE, SLOTS * NE, emit_codes, 0)
     lax.fori_loop(0, SLOTS * NE // 2, turn, 0)
     trunk_perm[...] = dot_tn(picker, trunk[...]).astype(BF16)
 
@@ -227,13 +232,15 @@
         hacc[rows, :] = dot(code[zh, rows, :], wfull[zh].reshape(HID // NZH, FEAT))
         return carry
 
-    lax.fori_loop(0, ROWS // HB, heads_first, 0)
+    lax.fori_loop(0, ROWS // HB // 2, heads_first, 0)
 
     for d in range(1, NX):
-        w_c[d - 1].wait()
+        for copies in w_c:
+            copies[d - 1].wait()
         cp = to_core(3 + d, (x + NX - d) % NX)
         cp.start()
         w_d.append(cp)
+    lax.fori_loop(ROWS // HB // 2, ROWS // HB, heads_first, 0)
     for cp in w_d:
         cp.wait()
 
@@ -261,58 +268,56 @@
         ex = jnp.where(valid, jnp.exp(lg - top), 0.0)
         probs[rows, :] = ex
         tops[pl.ds(s, 1), :] = top
-        st_send[s, 0:1, :] = top
-        st_send[s, 1:2, :] = jnp.sum(ex, axis=0, keepdims=True)
-        st_send[s, 2:3, :] = jnp.sum(jnp.where(onehot_of(s), lg, 0.0), axis=0, keepdims=True)
-        st_send[s, 3:4, :] = top
-        return carry
-
-    lax.fori_loop(0, SLOTS, logits_of, 0)
+        sums[pl.ds(s, 1), :] = jnp.sum(ex, axis=0, keepdims=True)
+        tg_send[pl.ds(s, 1), :] = jnp.sum(jnp.where(onehot_of(s), lg, 0.0), axis=0, keepdims=True)
+        return carry
+
+    hs = SLOTS // 2
+
+    def st_copies(g):
+        return [
+            remote(st_send.at[g], st_recv.at[g, d - 1], st_s.at[g, d - 1], st_r.at[g, d - 1], {"emit": (e + d) % NE})
+            for d in range(1, NE)
+        ]
 
     st = []
-    for d in range(1, NE):
-        to = (e + d) % NE
-        cp = remote(st_send.at[to], st_recv.at[d - 1], st_s.at[d - 1], st_r.at[d - 1], {"emit": to})
-        cp.start()
-        st.append(cp)
-
-    for cp in st:
-        cp.wait()
-    own_st = st_send[e]
-    every = [own_st] + [st_recv[d] for d in range(NE - 1)]
-    gtop = every[0][0:1]
-    for it in every[1:]:
-        gtop = jnp.maximum(gtop, it[0:1])
-    total = jnp.zeros_like(gtop)
-    target = jnp.zeros_like(gtop)
-    for it in every:
-        total += it[1:2] * jnp.exp(it[0:1] - gtop)
-        target += it[2:3]
-    logz = gtop + jnp.log(total)
-    res_send[0:1, :] = logz
-    res_send[1:2, :] = logz - target
-    rs = []
-    for d in range(1, NE):
-        cp = remote(res_send, res_recv.at[e], res_s.at[d - 1], res_r.at[d - 1], {"emit": (e + d) % NE})
-        cp.start()
-        rs.append(cp)
-    res_recv[e] = res_send[...]
-    for cp in rs:
-        cp.wait()
+    for g in range(2):
+        lax.fori_loop(g * hs, (g + 1) * hs, logits_of, 0, unroll=2)
+        st_send[g] = tops[g * hs : (g + 1) * hs, :] + jnp.log(sums[g * hs : (g + 1) * hs, :])
+        st.append(st_copies(g))
+        for cp in st[g]:
+            cp.start()
+
+    def combine(g):
+        for cp in st[g]:
+            cp.wait()
+        lse = st_send[g]
+        gtop = lse
+        for d in range(NE - 1):
+            gtop = jnp.maximum(gtop, st_recv[g, d])
+        total = jnp.exp(lse - gtop)
+        for d in range(NE - 1):
+            total += jnp.exp(st_recv[g, d] - gtop)
+        top = gtop + jnp.log(total)
+        part = slice(g * hs, (g + 1) * hs)
+        logz[part, :] = top
+        sums[part, :] = jnp.exp(tops[part, :] - top)
 
     def grads_of(s, carry):
         rows = pl.ds(pl.multiple_of(s * CPAD, CPAD), CPAD)
         frows = pl.ds(pl.multiple_of(s * SAMPLES, SAMPLES), SAMPLES)
-        scale = jnp.exp(tops[pl.ds(s, 1), :] - res_recv[s, 0:1, :])
-        g = probs[rows, :] * scale - onehot_of(s).astype(F32)
+        g = probs[rows, :] * sums[pl.ds(s, 1), :] - onehot_of(s).astype(F32)
         gh[rows, :] = dot((g * (1.0 / CLIENTS)).astype(BF16), feats[frows, :]).astype(BF16)
         return carry
 
-    lax.fori_loop(0, SLOTS, grads_of, 0)
-
-    for s in range(SLOTS):
-        for j in range(SAMPLES // 128):
-            loss_ref[s * 4 + j : s * 4 + j + 1, :] = res_recv[s, 1:2, j * 128 : (j + 1) * 128]
+    for g in range(2):
+        combine(g)
+        lax.fori_loop(g * hs, (g + 1) * hs, grads_of, 0, unroll=2)
+    tg = []
+    for d in range(1, NE):
+        cp = remote(tg_send, tg_recv.at[d - 1], res_s.at[d - 1], res_r.at[d - 1], {"emit": (e + d) % NE})
+        cp.start()
+        tg.append(cp)
 
     def core_copy(n):
         return remote(eg.at[n, 1 - core], egr.at[n], core_s.at[n], core_r.at[n], dev(core_=1 - core))
@@ -322,20 +327,31 @@
         part = pl.ds(pl.multiple_of(to * 32, 32), 32)
         return remote(am.at[2 * i, part], rx.at[i, d - 1], x1_s.at[i, d - 1], x1_r.at[i, d - 1], dev(x_=to))
 
+    def along_y(i):
+        return (y + 1 + 2 * i - 3 * (i // 2)) % NY
+
     def y1_copy(i):
-        return remote(am.at[2 * i + 1], ry.at[i], y1_s.at[i], y1_r.at[i], dev(y_=(y + 1 + i) % NY))
-
-    def compute_chunk(i):
-        yy = (y + 1 + i) % NY
-        for half in range(NZH):
+        return remote(am.at[2 * i + 1], ry.at[i], y1_s.at[i], y1_r.at[i], dev(y_=along_y(i)))
+
+    def compute_pair(i):
+        yy = along_y(i)
+        both = code_t[pl.ds(yy * NZH, NZH)].reshape(NZH * HB, ROWS)
+        part = dot(both, gh[...]).reshape(NZH, HB // (NK * 8), NK, 8, FEAT)
+        for half in (1, 0):
             n = 2 * i + half
-            part = dot(code_t[yy * NZH + half], gh[...]).reshape(16, NK, 8, FEAT)
             for k in range(NK):
-                eg[n, k] = part[:, k].reshape(HB // NK, FEAT).astype(BF16)
+                eg[n, k] = part[half, :, k].reshape(HB // NK, FEAT).astype(BF16)
             core_copy(n).start()
 
+    def sum_codes(h):
+        gc = dot_nt(gh[...], wfull[h % NZH, h // NZH])
+        lanes = pl.ds(pl.multiple_of(h * HB, HB), HB)
+        for s in range(SLOTS):
+            part = gc[s * CPAD : (s + 1) * CPAD] * dcode[s * CPAD : (s + 1) * CPAD, lanes].astype(F32)
+            gs_send[h, s : s + 1, :] = jnp.sum(part, axis=0, keepdims=True)
+
     def pass_on(i, last):
-        for half in range(NZH):
+        for half in (1, 0):
             n = 2 * i + half
             core_copy(n).wait()
             am[n] = (eg[n, core].astype(F32) + egr[n].astype(F32)).astype(BF16)
@@ -345,47 +361,46 @@
             elif not last:
                 y1_copy(i).start()
 
-    compute_chunk(0)
-
-    def chunk_step(i, carry):
-        compute_chunk(i)
-        pass_on(i - 1, False)
-        return carry
-
-    lax.fori_loop(1, NY, chunk_step, 0)
-
-    def sum_codes(h, carry):
-        gc = dot_nt(gh[...], wfull[h % NZH, h // NZH])
-        for s in range(SLOTS):
-            lanes = pl.ds(pl.multiple_of(h * HB, HB), HB)
-            part = gc[s * CPAD : (s + 1) * CPAD] * dcode[s * CPAD : (s + 1) * CPAD, lanes].astype(F32)
-            gs_send[h, s : s + 1, :] = jnp.sum(part, axis=0, keepdims=True)
-        return carry
-
-    lax.fori_loop(0, 1, sum_codes, 0)
-    pass_on(NY - 1, True)
-    lax.fori_loop(1, NE, sum_codes, 0)
-
-    gs = []
-    for d in range(1, NE):
-        to = (e + d) % NE
-        cp = remote(gs_send.at[to], gs_recv.at[d - 1], gs_s.at[d - 1], gs_r.at[d - 1], {"emit": to})
-        cp.start()
-        gs.append(cp)
+    def y2_copy(i):
+        return remote(bx.at[i], rxy.at[i], y2_s.at[i], y2_r.at[i], dev(y_=along_y(i)))
 
     xpart = pl.ds(pl.multiple_of(x * 32, 32), 32)
-    y2 = []
-    for i in range(NY):
+
+    def along_x_sum(i):
         for d in range(1, NX):
             x1_copy(i, d).wait()
         acc = am[2 * i, xpart, :].astype(F32)
         for d in range(NX - 1):
             acc += rx[i, d].astype(F32)
         bx[i] = acc.astype(BF16)
-        if i < NY - 1:
-            cp = remote(bx.at[i], rxy.at[i], y2_s.at[i], y2_r.at[i], dev(y_=(y + 1 + i) % NY))
-            cp.start()
-            y2.append(cp)
+
+    compute_pair(0)
+    sum_codes(0)
+
+    def chunk_step(i, carry):
+        compute_pair(i)
+        pass_on(i - 1, False)
+        sum_codes(i)
+        return carry
+
+    lax.fori_loop(1, NY, chunk_step, 0)
+    sum_codes(NY)
+    pass_on(NY - 1, True)
+
+    def second_step(i, carry):
+        sum_codes(NY + 1 + i)
+        along_x_sum(i)
+        y2_copy(i).start()
+        return carry
+
+    lax.fori_loop(0, NY - 1, second_step, 0)
+    gs = []
+    for d in range(1, NE):
+        to = (e + d) % NE
+        cp = remote(gs_send.at[to], gs_recv.at[d - 1], gs_s.at[d - 1], gs_r.at[d - 1], {"emit": to})
+        cp.start()
+        gs.append(cp)
+
     acc = am[2 * NY - 1].astype(F32)
     for i in range(NY - 1):
         y1_copy(i).wait()
@@ -398,6 +413,16 @@
         cp = remote(by.at[part], ryx.at[d - 1], x2_s.at[d - 1], x2_r.at[d - 1], dev(x_=to))
         cp.start()
         x2.append(cp)
+    along_x_sum(NY - 1)
+
+    for cp in tg:
+        cp.wait()
+    rest = logz[...] - tg_send[...]
+    for d in range(NE - 1):
+        rest = rest - tg_recv[d]
+    for s in range(SLOTS):
+        for j in range(SAMPLES // 128):
+            loss_ref[s * 4 + j : s * 4 + j + 1, :] = rest[s : s + 1, j * 128 : (j + 1) * 128]
 
     for cp in gs:
         cp.wait()
@@ -414,8 +439,8 @@
     own_gp = pltpu.make_async_copy(gp_send, gp_recv.at[c], gp_rsem)
     own_gp.start()
 
-    for cp in y2:
-        cp.wait()
+    for i in range(NY - 1):
+        y2_copy(i).wait()
     acc = bx[NY - 1].astype(F32)
     for d in range(NY - 1):
         acc += rxy[d].astype(F32)
@@ -470,7 +495,9 @@
         vm((NZH, ROWS, HID // NZH), BF16), vm((NE, HB, ROWS), BF16), vm((ROWS, HID), BF16), vm((ROWS, FEAT), F32),
         vm((ROWS, FEAT), BF16),
         vm((ROWS, SAMPLES), F32), vm((SLOTS, SAMPLES), F32),
-        vm((SLOTS, 4, SAMPLES), F32), vm((NE - 1, 4, SAMPLES), F32), vm((2, SAMPLES), F32), vm((SLOTS, 2, SAMPLES), F32),
+        vm((SLOTS, SAMPLES), F32), vm((SLOTS, SAMPLES), F32),
+        vm((2, SLOTS // 2, SAMPLES), F32), vm((2, NE - 1, SLOTS // 2, SAMPLES), F32), vm((SLOTS, SAMPLES), F32),
+        vm((NE - 1, SLOTS, SAMPLES), F32),
         vm((ROWS, FEAT), BF16), vm((NE, NK, half, FEAT), BF16), vm((NE, half, FEAT), BF16), vm((NE, half, FEAT), BF16),
         vm((NY, NX - 1, 32, FEAT), BF16), vm((NY - 1, half, FEAT), BF16),
         vm((NY, 32, FEAT), BF16), vm((NY - 1, 32, FEAT), BF16), vm((half, FEAT), BF16), vm((NX - 1, 32, FEAT), BF16),
@@ -478,8 +505,8 @@
         vm((NE, SLOTS, HB), F32), vm((NE - 1, SLOTS, HB), F32), vm((SLOTS, HB), BF16), vm((NC, SLOTS, HB), BF16),
         vm((CLIENTS, HID), BF16),
         dma((5,)), dma, dma,
-        dma((2, 3)), dma((2, 3)), dma, dma, dma((3,)), dma((3,)), dma((3,)), dma((3,)), dma((7,)), dma((7,)),
-        dma((7,)), dma((7,)), dma((7,)), dma((7,)), dma((8,)), dma((8,)),
+        dma((2, 3)), dma((2, 3)), dma, dma, dma((3,)), dma((3,)), dma((4, 3)), dma((4, 3)), dma((7,)), dma((7,)),
+        dma((2, 7)), dma((2, 7)), dma((7,)), dma((7,)), dma((8,)), dma((8,)),
         dma((4, 3)), dma((4, 3)), dma((3,)), dma((3,)), dma((3,)), dma((3,)), dma((3,)), dma((3,)), dma((7,)), dma((7,)),
         dma((7,)), dma((7,)), dma, dma,
     ]

time: 86.9 us -> 77.2 us (0.89); the launches traced: 85.2 us -> 76.4 us
  Pallas kernels: 84.6 us -> 75.7 us
    pallas_call x1, Pallas kernels: 83 us -> 74.2 us  [per_device(): pl.pallas_call(step_kernel, name='hyper_step', out_shape=(jax.ShapeDtypeS...]
where the time goes in v3:
time: 77.2 us; the launch traced here: 76.4 us
  Pallas kernels  75.7 us (98%)
    pallas_call x1, Pallas kernels, per_device(): pl.pallas_call(step_kernel, name='hyper_step', out_shape=(jax.ShapeDtypeS...  74.2 us

profile of v3, /device:TPU:1, one launch (start us, length us, event | category | flops | bytes accessed | tf_op | source)
XLA Modules:
  0.0 76.4 jit_solution(300839584072793671)
XLA Ops:
  0.6 74.2 %hyper_step.1 = (f32[32,128]{1,0:T(8,128)}, f32[8,768]{1,0:T(8,128)}, f32[8,2048]{1,0:T(8,128)}) custom-call(bf16[4096,768]{1,0:T(8,128)(2,1)} %feats_hbm.1, s32[32,128]{1,0:T(8,128)} %bitcast.6, s32[1,256]{1,0:T(1,128)} %bitcast.7, bf16[256,2048]{1,0:T(8,128)(2,1)} %trunk_hbm.1, bf16[64,2048]{1,0:T(8,128)(2,1)} %bitcast.5, bf16[125,2048]{1,0:T(8,128)(2,1)} %table_hbm.1, ...), custom_call_target="tpu_custom_call" | custom-call | tf_op jit(solution)/shard_map/hyper_step/pallas_call | solution.py:515
  74.8 1.5 %hand_over.1 = (f32[32,128]{1,0:T(8,128)}, f32[8,768]{1,0:T(8,128)}, f32[8,2048]{1,0:T(8,128)}) custom-call(f32[32,128]{1,0:T(8,128)} %get-tuple-element.9.loss_in, f32[8,768]{1,0:T(8,128)} %get-tuple-element.10.egrad_in, f32[8,2048]{1,0:T(8,128)} %get-tuple-element.11.tgrad_in), custom_call_target="tpu_custom_call" | custom-call | tf_op jit(solution)/shard_map/hand_over/pallas_call | solution.py:532

commit v4 on v3

--- a/solution.py
+++ b/solution.py
@@ -333,15 +333,12 @@
     def y1_copy(i):
         return remote(am.at[2 * i + 1], ry.at[i], y1_s.at[i], y1_r.at[i], dev(y_=along_y(i)))
 
-    def compute_pair(i):
-        yy = along_y(i)
-        both = code_t[pl.ds(yy * NZH, NZH)].reshape(NZH * HB, ROWS)
-        part = dot(both, gh[...]).reshape(NZH, HB // (NK * 8), NK, 8, FEAT)
-        for half in (1, 0):
-            n = 2 * i + half
-            for k in range(NK):
-                eg[n, k] = part[half, :, k].reshape(HB // NK, FEAT).astype(BF16)
-            core_copy(n).start()
+    def compute_chunk(i, half):
+        n = 2 * i + half
+        part = dot(code_t[along_y(i) * NZH + half], gh[...]).reshape(HB // (NK * 8), NK, 8, FEAT)
+        for k in range(NK):
+            eg[n, k] = part[:, k].reshape(HB // NK, FEAT).astype(BF16)
+        core_copy(n).start()
 
     def sum_codes(h):
         gc = dot_nt(gh[...], wfull[h % NZH, h // NZH])
@@ -350,16 +347,17 @@
             part = gc[s * CPAD : (s + 1) * CPAD] * dcode[s * CPAD : (s + 1) * CPAD, lanes].astype(F32)
             gs_send[h, s : s + 1, :] = jnp.sum(part, axis=0, keepdims=True)
 
-    def pass_on(i, last):
-        for half in (1, 0):
-            n = 2 * i + half
-            core_copy(n).wait()
-            am[n] = (eg[n, core].astype(F32) + egr[n].astype(F32)).astype(BF16)
-            if half == 0:
-                for d in range(1, NX):
-                    x1_copy(i, d).start()
-            elif not last:
-                y1_copy(i).start()
+    def pass_on(i, half):
+        n = 2 * i + half
+        core_copy(n).wait()
+        am[n] = (eg[n, core].astype(F32) + egr[n].astype(F32)).astype(BF16)
+        if half == 0:
+            for d in range(1, NX):
+                x1_copy(i, d).start()
+
+    def pass_on_y(i):
+        pass_on(i, 1)
+        y1_copy(i).start()
 
     def y2_copy(i):
         return remote(bx.at[i], rxy.at[i], y2_s.at[i], y2_r.at[i], dev(y_=along_y(i)))
@@ -374,26 +372,32 @@
             acc += rx[i, d].astype(F32)
         bx[i] = acc.astype(BF16)
 
-    compute_pair(0)
+    compute_chunk(0, 1)
+    compute_chunk(0, 0)
+    compute_chunk(1, 1)
+
+    def chunk_step(j, carry):
+        compute_chunk(j + 1, 0)
+        pass_on_y(j)
+        compute_chunk(j + 2, 1)
+        pass_on(j, 0)
+        return carry
+
+    lax.fori_loop(0, NY - 2, chunk_step, 0)
+    compute_chunk(NY - 1, 0)
+    pass_on_y(NY - 2)
     sum_codes(0)
-
-    def chunk_step(i, carry):
-        compute_pair(i)
-        pass_on(i - 1, False)
-        sum_codes(i)
-        return carry
-
-    lax.fori_loop(1, NY, chunk_step, 0)
-    sum_codes(NY)
-    pass_on(NY - 1, True)
-
-    def second_step(i, carry):
-        sum_codes(NY + 1 + i)
-        along_x_sum(i)
-        y2_copy(i).start()
-        return carry
-
-    lax.fori_loop(0, NY - 1, second_step, 0)
+    pass_on(NY - 2, 0)
+    sum_codes(1)
+    pass_on(NY - 1, 0)
+    pass_on(NY - 1, 1)
+
+    def sum_step(h, carry):
+        sum_codes(h)
+        return carry
+
+    lax.fori_loop(2, NE, sum_step, 0)
+
     gs = []
     for d in range(1, NE):
         to = (e + d) % NE
@@ -401,6 +405,12 @@
         cp.start()
         gs.append(cp)
 
+    def second_step(i, carry):
+        along_x_sum(i)
+        y2_copy(i).start()
+        return carry
+
+    lax.fori_loop(0, NY - 1, second_step, 0)
     acc = am[2 * NY - 1].astype(F32)
     for i in range(NY - 1):
         y1_copy(i).wait()
@@ -414,15 +424,6 @@
         cp.start()
         x2.append(cp)
     along_x_sum(NY - 1)
-
-    for cp in tg:
-        cp.wait()
-    rest = logz[...] - tg_send[...]
-    for d in range(NE - 1):
-        rest = rest - tg_recv[d]
-    for s in range(SLOTS):
-        for j in range(SAMPLES // 128):
-            loss_ref[s * 4 + j : s * 4 + j + 1, :] = rest[s : s + 1, j * 128 : (j + 1) * 128]
 
     for cp in gs:
         cp.wait()
@@ -458,6 +459,15 @@
         cp = remote(cz.at[to], rz.at[d - 1], z_s.at[d - 1], z_r.at[d - 1], dev(z_=to))
         cp.start()
         zs.append(cp)
+
+    for cp in tg:
+        cp.wait()
+    rest = logz[...] - tg_send[...]
+    for d in range(NE - 1):
+        rest = rest - tg_recv[d]
+    for s in range(SLOTS):
+        for j in range(SAMPLES // 128):
+            loss_ref[s * 4 + j : s * 4 + j + 1, :] = rest[s : s + 1, j * 128 : (j + 1) * 128]
 
     pltpu.make_async_copy(gp_recv, gp_recv, gp_rsem).wait()
     select = (

time: 77.2 us -> 75.3 us (0.975)
  Pallas kernels: 75.7 us -> 74.5 us
    pallas_call x1, Pallas kernels: 74.2 us -> 72.9 us  [per_device(): pl.pallas_call(step_kernel, name='hyper_step', out_shape=(jax.ShapeDtypeS...]
where the time goes in v4:
time: 75.3 us; the launch traced here: 75.1 us
  Pallas kernels  74.5 us (99%)
    pallas_call x1, Pallas kernels, per_device(): pl.pallas_call(step_kernel, name='hyper_step', out_shape=(jax.ShapeDtypeS...  72.9 us
    pallas_call x1, Pallas kernels, per_device(): pl.pallas_call(hand_over, name='hand_over', out_shape=tuple((jax.ShapeDty...  1.52 us

profile of v4, /device:TPU:1, one launch (start us, length us, event | category | flops | bytes accessed | tf_op | source)
XLA Modules:
  0.0 75.1 jit_solution(3633713925893947584)
XLA Ops:
  0.6 72.9 %hyper_step.1 = (f32[32,128]{1,0:T(8,128)}, f32[8,768]{1,0:T(8,128)}, f32[8,2048]{1,0:T(8,128)}) custom-call(bf16[4096,768]{1,0:T(8,128)(2,1)} %feats_hbm.1, s32[32,128]{1,0:T(8,128)} %bitcast.6, s32[1,256]{1,0:T(1,128)} %bitcast.7, bf16[256,2048]{1,0:T(8,128)(2,1)} %trunk_hbm.1, bf16[64,2048]{1,0:T(8,128)(2,1)} %bitcast.5, bf16[125,2048]{1,0:T(8,128)(2,1)} %table_hbm.1, ...), custom_call_target="tpu_custom_call" | custom-call | tf_op jit(solution)/shard_map/hyper_step/pallas_call | solution.py:525
  73.6 1.5 %hand_over.1 = (f32[32,128]{1,0:T(8,128)}, f32[8,768]{1,0:T(8,128)}, f32[8,2048]{1,0:T(8,128)}) custom-call(f32[32,128]{1,0:T(8,128)} %get-tuple-element.9.loss_in, f32[8,768]{1,0:T(8,128)} %get-tuple-element.10.egrad_in, f32[8,2048]{1,0:T(8,128)} %get-tuple-element.11.tgrad_in), custom_call_target="tpu_custom_call" | custom-call | tf_op jit(solution)/shard_map/hand_over/pallas_call | solution.py:542

commit v5 on v4

--- a/solution.py
+++ b/solution.py
@@ -13,6 +13,7 @@
 NE, NC = NY * NZH, NX * NZL * NK
 SLOTS = 8
 SAMPLES = 512
+GROUPS = 4
 CPAD = 128
 ROWS = SLOTS * CPAD
 HID = 2048
@@ -46,7 +47,7 @@
     code, code_t, dcode, hacc, heads, probs, tops,
     sums, logz, st_send, st_recv, tg_send, tg_recv,
     gh, eg, egr, am, rx, ry, bx, rxy, by, ryx, cz, rz,
-    gs_send, gs_recv, gp_send, gp_recv, trunk_perm,
+    gs_send, gs_half, gs_recv, gp_send, gp_recv, trunk_perm,
     loc_sem, pre_ssem, pre_rsem,
     wa_s, wa_r, wz_s, wz_r, wb_s, wb_r, wc_s, wc_r, wd_s, wd_r,
     st_s, st_r, res_s, res_r, core_s, core_r,
@@ -272,7 +273,7 @@
         tg_send[pl.ds(s, 1), :] = jnp.sum(jnp.where(onehot_of(s), lg, 0.0), axis=0, keepdims=True)
         return carry
 
-    hs = SLOTS // 2
+    hs = SLOTS // GROUPS
 
     def st_copies(g):
         return [
@@ -281,7 +282,7 @@
         ]
 
     st = []
-    for g in range(2):
+    for g in range(GROUPS):
         lax.fori_loop(g * hs, (g + 1) * hs, logits_of, 0, unroll=2)
         st_send[g] = tops[g * hs : (g + 1) * hs, :] + jnp.log(sums[g * hs : (g + 1) * hs, :])
         st.append(st_copies(g))
@@ -310,7 +311,7 @@
         gh[rows, :] = dot((g * (1.0 / CLIENTS)).astype(BF16), feats[frows, :]).astype(BF16)
         return carry
 
-    for g in range(2):
+    for g in range(GROUPS):
         combine(g)
         lax.fori_loop(g * hs, (g + 1) * hs, grads_of, 0, unroll=2)
     tg = []
@@ -372,45 +373,40 @@
             acc += rx[i, d].astype(F32)
         bx[i] = acc.astype(BF16)
 
-    compute_chunk(0, 1)
-    compute_chunk(0, 0)
-    compute_chunk(1, 1)
-
-    def chunk_step(j, carry):
-        compute_chunk(j + 1, 0)
+    def first_chunks(j, carry):
+        compute_chunk(j, 1)
+        return carry
+
+    def next_chunks(j, carry):
+        compute_chunk(j, 0)
         pass_on_y(j)
-        compute_chunk(j + 2, 1)
-        pass_on(j, 0)
-        return carry
-
-    lax.fori_loop(0, NY - 2, chunk_step, 0)
-    compute_chunk(NY - 1, 0)
-    pass_on_y(NY - 2)
-    sum_codes(0)
-    pass_on(NY - 2, 0)
-    sum_codes(1)
-    pass_on(NY - 1, 0)
-    pass_on(NY - 1, 1)
+        return carry
 
     def sum_step(h, carry):
         sum_codes(h)
         return carry
 
+    lax.fori_loop(0, NY - 1, first_chunks, 0)
+    lax.fori_loop(0, NY - 1, next_chunks, 0)
+    compute_chunk(NY - 1, 0)
+    pass_on(0, 0)
+    compute_chunk(NY - 1, 1)
+    pass_on(1, 0)
+    sum_codes(0)
+    pass_on(2, 0)
+    sum_codes(1)
+    pass_on(3, 0)
+    pass_on(3, 1)
     lax.fori_loop(2, NE, sum_step, 0)
 
+    gs_half[...] = gs_send[...].astype(BF16)
     gs = []
     for d in range(1, NE):
         to = (e + d) % NE
-        cp = remote(gs_send.at[to], gs_recv.at[d - 1], gs_s.at[d - 1], gs_r.at[d - 1], {"emit": to})
+        cp = remote(gs_half.at[to], gs_recv.at[d - 1], gs_s.at[d - 1], gs_r.at[d - 1], {"emit": to})
         cp.start()
         gs.append(cp)
 
-    def second_step(i, carry):
-        along_x_sum(i)
-        y2_copy(i).start()
-        return carry
-
-    lax.fori_loop(0, NY - 1, second_step, 0)
     acc = am[2 * NY - 1].astype(F32)
     for i in range(NY - 1):
         y1_copy(i).wait()
@@ -423,13 +419,18 @@
         cp = remote(by.at[part], ryx.at[d - 1], x2_s.at[d - 1], x2_r.at[d - 1], dev(x_=to))
         cp.start()
         x2.append(cp)
-    along_x_sum(NY - 1)
+    def second_step(i, carry):
+        along_x_sum(i)
+        y2_copy(i).start()
+        return carry
+
+    lax.fori_loop(0, NY - 1, second_step, 0)
 
     for cp in gs:
         cp.wait()
     block = gs_send[e]
     for d in range(NE - 1):
-        block = block + gs_recv[d]
+        block = block + gs_recv[d].astype(F32)
     gp_send[...] = (block * dpre[e]).astype(BF16)
 
     def send_gp(d, carry):
@@ -440,6 +441,7 @@
     own_gp = pltpu.make_async_copy(gp_send, gp_recv.at[c], gp_rsem)
     own_gp.start()
 
+    along_x_sum(NY - 1)
     for i in range(NY - 1):
         y2_copy(i).wait()
     acc = bx[NY - 1].astype(F32)
@@ -506,17 +508,17 @@
         vm((ROWS, FEAT), BF16),
         vm((ROWS, SAMPLES), F32), vm((SLOTS, SAMPLES), F32),
         vm((SLOTS, SAMPLES), F32), vm((SLOTS, SAMPLES), F32),
-        vm((2, SLOTS // 2, SAMPLES), F32), vm((2, NE - 1, SLOTS // 2, SAMPLES), F32), vm((SLOTS, SAMPLES), F32),
+        vm((GROUPS, SLOTS // GROUPS, SAMPLES), F32), vm((GROUPS, NE - 1, SLOTS // GROUPS, SAMPLES), F32), vm((SLOTS, SAMPLES), F32),
         vm((NE - 1, SLOTS, SAMPLES), F32),
         vm((ROWS, FEAT), BF16), vm((NE, NK, half, FEAT), BF16), vm((NE, half, FEAT), BF16), vm((NE, half, FEAT), BF16),
         vm((NY, NX - 1, 32, FEAT), BF16), vm((NY - 1, half, FEAT), BF16),
         vm((NY, 32, FEAT), BF16), vm((NY - 1, 32, FEAT), BF16), vm((half, FEAT), BF16), vm((NX - 1, 32, FEAT), BF16),
         vm((NZH * NZL, 8, FEAT), BF16), vm((NZH * NZL - 1, 8, FEAT), BF16),
-        vm((NE, SLOTS, HB), F32), vm((NE - 1, SLOTS, HB), F32), vm((SLOTS, HB), BF16), vm((NC, SLOTS, HB), BF16),
+        vm((NE, SLOTS, HB), F32), vm((NE, SLOTS, HB), BF16), vm((NE - 1, SLOTS, HB), BF16), vm((SLOTS, HB), BF16), vm((NC, SLOTS, HB), BF16),
         vm((CLIENTS, HID), BF16),
         dma((5,)), dma, dma,
         dma((2, 3)), dma((2, 3)), dma, dma, dma((3,)), dma((3,)), dma((4, 3)), dma((4, 3)), dma((7,)), dma((7,)),
-        dma((2, 7)), dma((2, 7)), dma((7,)), dma((7,)), dma((8,)), dma((8,)),
+        dma((GROUPS, 7)), dma((GROUPS, 7)), dma((7,)), dma((7,)), dma((8,)), dma((8,)),
         dma((4, 3)), dma((4, 3)), dma((3,)), dma((3,)), dma((3,)), dma((3,)), dma((3,)), dma((3,)), dma((7,)), dma((7,)),
         dma((7,)), dma((7,)), dma, dma,
     ]

time: 75.3 us -> 74 us (0.983)
  Pallas kernels: 74.5 us -> 73.2 us
    pallas_call x1, Pallas kernels: 72.9 us -> 71.7 us  [per_device(): pl.pallas_call(step_kernel, name='hyper_step', out_shape=(jax.ShapeDtypeS...]
where the time goes in v5:
time: 74 us; the launch traced here: 73.9 us
  Pallas kernels  73.2 us (99%)
    pallas_call x1, Pallas kernels, per_device(): pl.pallas_call(step_kernel, name='hyper_step', out_shape=(jax.ShapeDtypeS...  71.7 us
    pallas_call x1, Pallas kernels, per_device(): pl.pallas_call(hand_over, name='hand_over', out_shape=tuple((jax.ShapeDty...  1.52 us

profile of v5, /device:TPU:1, one launch (start us, length us, event | category | flops | bytes accessed | tf_op | source)
XLA Modules:
  0.0 73.9 jit_solution(13220243738493598931)
XLA Ops:
  0.6 71.7 %hyper_step.1 = (f32[32,128]{1,0:T(8,128)}, f32[8,768]{1,0:T(8,128)}, f32[8,2048]{1,0:T(8,128)}) custom-call(bf16[4096,768]{1,0:T(8,128)(2,1)} %feats_hbm.1, s32[32,128]{1,0:T(8,128)} %bitcast.6, s32[1,256]{1,0:T(1,128)} %bitcast.7, bf16[256,2048]{1,0:T(8,128)(2,1)} %trunk_hbm.1, bf16[64,2048]{1,0:T(8,128)(2,1)} %bitcast.5, bf16[125,2048]{1,0:T(8,128)(2,1)} %table_hbm.1, ...), custom_call_target="tpu_custom_call" | custom-call | tf_op jit(solution)/shard_map/hyper_step/pallas_call | solution.py:527
  72.3 1.5 %hand_over.1 = (f32[32,128]{1,0:T(8,128)}, f32[8,768]{1,0:T(8,128)}, f32[8,2048]{1,0:T(8,128)}) custom-call(f32[32,128]{1,0:T(8,128)} %get-tuple-element.9.loss_in, f32[8,768]{1,0:T(8,128)} %get-tuple-element.10.egrad_in, f32[8,2048]{1,0:T(8,128)} %get-tuple-element.11.tgrad_in), custom_call_target="tpu_custom_call" | custom-call | tf_op jit(solution)/shard_map/hand_over/pallas_call | solution.py:544

commit v6 on v5

--- a/solution.py
+++ b/solution.py
@@ -229,11 +229,11 @@
         cp.wait()
 
     def heads_first(m, carry):
-        rows = pl.ds(pl.multiple_of(m * HB, HB), HB)
+        rows = pl.ds(pl.multiple_of(m * 2 * HB, 2 * HB), 2 * HB)
         hacc[rows, :] = dot(code[zh, rows, :], wfull[zh].reshape(HID // NZH, FEAT))
         return carry
 
-    lax.fori_loop(0, ROWS // HB // 2, heads_first, 0)
+    lax.fori_loop(0, ROWS // HB // 4, heads_first, 0)
 
     for d in range(1, NX):
         for copies in w_c:
@@ -241,17 +241,17 @@
         cp = to_core(3 + d, (x + NX - d) % NX)
         cp.start()
         w_d.append(cp)
-    lax.fori_loop(ROWS // HB // 2, ROWS // HB, heads_first, 0)
+    lax.fori_loop(ROWS // HB // 4, ROWS // HB // 2, heads_first, 0)
     for cp in w_d:
         cp.wait()
 
     def heads_rest(m, carry):
-        rows = pl.ds(pl.multiple_of(m * HB, HB), HB)
+        rows = pl.ds(pl.multiple_of(m * 2 * HB, 2 * HB), 2 * HB)
         part = dot(code[1 - zh, rows, :], wfull[1 - zh].reshape(HID // NZH, FEAT))
         heads[rows, :] = (hacc[rows, :] + part).astype(BF16)
         return carry
 
-    lax.fori_loop(0, ROWS // HB, heads_rest, 0)
+    lax.fori_loop(0, ROWS // HB // 2, heads_rest, 0)
     ld_feats.wait()
 
     kids = lax.broadcasted_iota(jnp.int32, (CPAD, SAMPLES), 0)

time: 74 us -> 73.8 us (level)
  no operation moved by 1% of the time
where the time goes in v6:
time: 73.8 us; the launch traced here: 73.6 us
  Pallas kernels  73 us (99%)
    pallas_call x1, Pallas kernels, per_device(): pl.pallas_call(step_kernel, name='hyper_step', out_shape=(jax.ShapeDtypeS...  71.4 us
    pallas_call x1, Pallas kernels, per_device(): pl.pallas_call(hand_over, name='hand_over', out_shape=tuple((jax.ShapeDty...  1.52 us

profile of v6, /device:TPU:1, one launch (start us, length us, event | category | flops | bytes accessed | tf_op | source)
XLA Modules:
  0.0 73.6 jit_solution(15698913636796897007)
XLA Ops:
  0.6 71.4 %hyper_step.1 = (f32[32,128]{1,0:T(8,128)}, f32[8,768]{1,0:T(8,128)}, f32[8,2048]{1,0:T(8,128)}) custom-call(bf16[4096,768]{1,0:T(8,128)(2,1)} %feats_hbm.1, s32[32,128]{1,0:T(8,128)} %bitcast.6, s32[1,256]{1,0:T(1,128)} %bitcast.7, bf16[256,2048]{1,0:T(8,128)(2,1)} %trunk_hbm.1, bf16[64,2048]{1,0:T(8,128)(2,1)} %bitcast.5, bf16[125,2048]{1,0:T(8,128)(2,1)} %table_hbm.1, ...), custom_call_target="tpu_custom_call" | custom-call | tf_op jit(solution)/shard_map/hyper_step/pallas_call | solution.py:527
  72.1 1.5 %hand_over.1 = (f32[32,128]{1,0:T(8,128)}, f32[8,768]{1,0:T(8,128)}, f32[8,2048]{1,0:T(8,128)}) custom-call(f32[32,128]{1,0:T(8,128)} %get-tuple-element.9.loss_in, f32[8,768]{1,0:T(8,128)} %get-tuple-element.10.egrad_in, f32[8,2048]{1,0:T(8,128)} %get-tuple-element.11.tgrad_in), custom_call_target="tpu_custom_call" | custom-call | tf_op jit(solution)/shard_map/hand_over/pallas_call | solution.py:544
